TPU v7x, 512 devices: a whole 4x8x8 slice. The times are simulated.
512 devices in a mesh: dom: 128 (over y, z, core), rep: 4 (over x).
Axes of the slice: x: 4, y: 8, z: 8, core: 2. Of those that a mesh axis runs over, the one named last changes fastest.
Arguments:
- features: bfloat16 [32768, 1024], P('dom', 'rep'), may hold values from -6 to 6
- w_self: bfloat16 [1024, 1024], P('rep'), may hold values from -0.1875 to 0.1875
- w_neigh: bfloat16 [1024, 1024], P('rep'), may hold values from -0.1875 to 0.1875
- grad_out: bfloat16 [32768, 1024], P('dom', 'rep'), may hold values from -6 to 6
- mirror_list: int32 [16384, 4], P('dom'), may hold values from 0 to 255, as said below
- mirror_count: int32 [16384], P('dom'), may hold values from 1 to 4, as said below
- tile_dst: int32 [1024], P('dom'), may hold values from 0 to 1
- tile_src: int32 [1024], P('dom'), may hold values from 0 to 5
- tiles: bfloat16 [1024, 128, 128], P('dom'), may hold values from 0 to 4, as said below
Outputs:
- hidden_out: bfloat16 [32768, 1024], P('dom', 'rep')
- grad_features: bfloat16 [32768, 1024], P('dom', 'rep')
- grad_self: bfloat16 [1024, 1024], P('rep')
- grad_neigh: bfloat16 [1024, 1024], P('rep')
Inputs may be any that keep to these rules, and one draw needn't show every extreme that they name: `mirror_list`: the entries of one row are distinct. `mirror_count`: every partition has a peer whose count is exactly 4. Weights are zero in columns that fall on unused mirror slots; on each partition the slots after its live tiles hold zeros, and some partition has all 8 slots live.
All inputs are finite; a program needn't handle non-finite values.
Results may differ from a plain program's by a relative error of at most 0.0058.
Values may be sent and summed in bfloat16 or wider, within the bound.
A program may use at most 64 MiB of HBM per device.

v0:
```python
import jax
import jax.numpy as jnp
from jax import lax
from jax.sharding import PartitionSpec as P


def local(
    features, w_self, w_neigh, grad_out, mirror_list, mirror_count, tile_dst, tile_src, tiles
):
    highest = lax.Precision.HIGHEST
    rows_dev, col_width = features.shape
    dom_count = lax.axis_size("dom")
    slot_count = mirror_list.shape[1]
    tile_rows = tiles.shape[1]
    mirrors_dev = dom_count * slot_count
    src_count = (rows_dev + mirrors_dev) // tile_rows
    dst_count = rows_dev // tile_rows
    live_mask = jnp.arange(slot_count, dtype=jnp.int32)[None, :] < mirror_count[:, None]
    flat_list = mirror_list.reshape(-1)
    outgoing = jnp.where(
        live_mask[:, :, None], features[flat_list].reshape(dom_count, slot_count, col_width), 0
    )
    incoming = lax.all_to_all(outgoing, "dom", split_axis=0, concat_axis=0, tiled=True)
    row_table = jnp.concatenate([features, incoming.reshape(mirrors_dev, col_width)], axis=0)
    dst_onehot = (tile_dst[None, :] == jnp.arange(dst_count, dtype=jnp.int32)[:, None]).astype(
        jnp.float32
    )
    src_onehot = (tile_src[None, :] == jnp.arange(src_count, dtype=jnp.int32)[:, None]).astype(
        jnp.float32
    )
    gathered = row_table.reshape(src_count, tile_rows, col_width)[tile_src]
    contrib = jnp.einsum("tij,tjd->tid", tiles, gathered, preferred_element_type=jnp.float32)
    summed = jnp.einsum("st,tid->sid", dst_onehot, contrib, precision=highest).reshape(
        rows_dev, col_width
    )
    row_weight = jnp.sum(tiles, axis=2, dtype=jnp.float32)
    degree = jnp.einsum("st,ti->si", dst_onehot, row_weight, precision=highest).reshape(rows_dev)
    safe_degree = jnp.maximum(degree, 1.0)[:, None]
    aggregated = (summed / safe_degree).astype(jnp.bfloat16)
    partial_value = jnp.dot(features, w_self, preferred_element_type=jnp.float32) + jnp.dot(
        aggregated, w_neigh, preferred_element_type=jnp.float32
    )
    pre_act = lax.psum_scatter(partial_value, "rep", scatter_dimension=1, tiled=True)
    gate_sig = jax.nn.sigmoid(pre_act)
    hidden_out = (pre_act * gate_sig).astype(jnp.bfloat16)
    grad_pre = (
        grad_out.astype(jnp.float32) * (gate_sig + pre_act * gate_sig * (1.0 - gate_sig))
    ).astype(jnp.bfloat16)
    grad_full = lax.all_gather(grad_pre, "rep", axis=1, tiled=True)
    contract_rows = (((0,), (0,)), ((), ()))
    local_self = lax.dot_general(
        features, grad_full, contract_rows, preferred_element_type=jnp.float32
    )
    local_neigh = lax.dot_general(
        aggregated, grad_full, contract_rows, preferred_element_type=jnp.float32
    )
    grad_scale = float(rows_dev * dom_count) ** (-0.5)
    sum_self, sum_neigh = lax.psum((local_self, local_neigh), "dom")
    out_self = (sum_self * grad_scale).astype(jnp.bfloat16)
    out_neigh = (sum_neigh * grad_scale).astype(jnp.bfloat16)
    contract_cols = (((1,), (1,)), ((), ()))
    direct = lax.dot_general(grad_full, w_self, contract_cols, preferred_element_type=jnp.float32)
    grad_agg = (
        lax.dot_general(grad_full, w_neigh, contract_cols, preferred_element_type=jnp.float32)
        / safe_degree
    ).astype(jnp.bfloat16)
    grad_tiles = grad_agg.reshape(dst_count, tile_rows, col_width)[tile_dst]
    back_contrib = jnp.einsum("tij,tid->tjd", tiles, grad_tiles, preferred_element_type=jnp.float32)
    table_grad = jnp.einsum("st,tjd->sjd", src_onehot, back_contrib, precision=highest).reshape(
        src_count * tile_rows, col_width
    )
    mirror_grad = table_grad[rows_dev:].reshape(dom_count, slot_count, col_width)
    returned = lax.all_to_all(mirror_grad, "dom", split_axis=0, concat_axis=0, tiled=True)
    returned = jnp.where(live_mask[:, :, None], returned, jnp.float32(0.0))
    grad_total = direct + table_grad[:rows_dev]
    grad_total = grad_total.at[flat_list].add(returned.reshape(mirrors_dev, col_width))
    return (hidden_out, grad_total.astype(jnp.bfloat16), out_self, out_neigh)


def solution(mesh):
    in_specs = (
        P("dom", "rep"),
        P("rep", None),
        P("rep", None),
        P("dom", "rep"),
        P("dom", None),
        P("dom"),
        P("dom"),
        P("dom"),
        P("dom", None, None),
    )
    out_specs = (P("dom", "rep"), P("dom", "rep"), P("rep", None), P("rep", None))
    return jax.shard_map(local, mesh=mesh, in_specs=in_specs, out_specs=out_specs, check_vma=False)
```

profile of v0, /device:TPU:1, one launch (start us, length us, event | category | flops | bytes accessed | tf_op | source)
XLA Modules:
  0.0 319.5 jit_solution(13757081189725662472)
XLA Ops:
  7.2 0.8 iota_compare_fusion
  8.3 0.6 copy-done.7
  8.8 2.0 gather_fusion
  10.9 0.9 broadcast_select_fusion.1
  11.8 18.6 %all-to-all-start = ((bf16[128,4,256]{2,1,0:T(4,128)(2,1)}), bf16[128,4,256]{2,1,0:T(4,128)(2,1)S(1)}, u32[]{:S(2)}, u32[]{:S(2)}) async-start(bf16[128,4,256]{2,1,0:T(4,128)(2,1)} %broadcast_select_fusion.1), calls=%async_computation | async-start | bytes 524288 | tf_op jit(solution)/shard_map/all_to_all | solution.py:23
  30.6 0.5 copy-done.9
  31.3 1.3 fusion.15
  32.6 12.1 %all-to-all-done = bf16[128,4,256]{2,1,0:T(4,128)(2,1)S(1)} async-done(((bf16[128,4,256]{2,1,0:T(4,128)(2,1)}), bf16[128,4,256]{2,1,0:T(4,128)(2,1)S(1)}, u32[]{:S(2)}, u32[]{:S(2)}) %all-to-all-start) | async-done | bytes 262176 | tf_op jit(solution)/shard_map/all_to_all | solution.py:23
  44.7 0.6 gather_fusion.1
  45.7 0.5 copy.24
  46.2 0.6 fusion.4
  46.9 0.5 copy-done.2
  47.4 1.3 convolution_add_fusion
  48.7 20.8 %reduce-scatter.2.cloned.1.call-done = f32[256,256]{1,0:T(8,128)} async-done(((f32[256,1024]{1,0:T(8,128)}), f32[256,256]{1,0:T(8,128)}) %reduce-scatter.2.cloned.1.call-update) | async-done | bytes 262160 | tf_op jit(solution)/shard_map/reduce_scatter | solution.py:43
  69.5 1.7 multiply_convert_fusion.2
  71.2 10.8 %all_gather.3 = bf16[256,1024]{1,0:T(8,128)(2,1)S(1)} all-gather(bf16[256,256]{1,0:T(8,128)(2,1)S(1)} %get-tuple-element.14), channel_id=1, replica_groups=mesh['dom'=128,'rep'=4] {'rep'}, dimensions={1}, use_global_device_ids=true | all-gather | bytes 655360 | tf_op jit(solution)/shard_map/all_gather | solution.py:49
  82.4 1.4 fusion.18
  83.8 0.6 gather_fusion.2
  84.7 0.5 copy.25
  85.4 0.6 fusion.2
  86.2 0.9 reshape.101
  87.2 17.6 %all-to-all-start.1 = ((f32[128,4,256]{2,1,0:T(4,128)}), f32[128,4,256]{2,1,0:T(4,128)S(1)}, u32[]{:S(2)}, u32[]{:S(2)}) async-start(f32[128,4,256]{2,1,0:T(4,128)} %reshape.101), calls=%async_computation.2 | async-start | bytes 1048576 | tf_op jit(solution)/shard_map/all_to_all | solution.py:73
  104.8 1.3 convolution_bitcast_fusion
  106.3 0.9 copy-done.5
  107.6 16.7 %all-to-all-done.1 = f32[128,4,256]{2,1,0:T(4,128)S(1)} async-done(((f32[128,4,256]{2,1,0:T(4,128)}), f32[128,4,256]{2,1,0:T(4,128)S(1)}, u32[]{:S(2)}, u32[]{:S(2)}) %all-to-all-start.1) | async-done | bytes 524320 | tf_op jit(solution)/shard_map/all_to_all | solution.py:73
  124.6 0.5 copy-done.8
  125.1 3.6 %scatter_fusion = f32[256,256]{1,0:T(8,128)S(1)} fusion(f32[256,256]{1,0:T(8,128)S(1)} %convolution_add_fusion.1, s32[512]{0:T(512)S(1)} %bitcast.45, f32[512,256]{1,0:T(8,128)S(1)} %reshape.131), kind=kCustom, calls=%fused_computation.3 | custom fusion | flops 131072 | bytes 1574912 | tf_op jit(solution)/shard_map/scatter-add | solution.py:76
  128.8 0.7 convert_element_type.37
  129.4 179.4 %all-reduce.3.cloned.1.call-done = (f32[256,1024]{0,1:T(8,128)}, f32[256,1024]{0,1:T(8,128)}) async-done(((f32[256,1024]{0,1:T(8,128)}, f32[256,1024]{0,1:T(8,128)}), (f32[256,1024]{0,1:T(8,128)}, f32[256,1024]{0,1:T(8,128)})) %all-reduce.3.cloned.1.call-update) | async-done | bytes 2097168 | tf_op jit(solution)/shard_map/psum | solution.py:58
  308.9 1.8 multiply_convert_fusion
  310.6 1.0 copy.23
  311.6 1.0 copy.22
  (50 shorter events, 3.3 us)
Async XLA Ops:
  7.2 39.7 %copy-start = (bf16[256,1024]{1,0:T(8,128)(2,1)S(1)}, bf16[256,1024]{1,0:T(8,128)(2,1)}, u32[]{:S(2)}) copy-start(bf16[256,1024]{1,0:T(8,128)(2,1)} %param.11) | copy-start | bytes 1572868
  7.2 0.8 copy-start.10
  7.2 1.6 copy-start.1
  8.2 0.6 copy-start.7
  10.9 19.6 %copy-start.11 = (s32[8]{0:T(128)S(1)}, s32[8]{0:T(128)}, u32[]{:S(2)}) copy-start(s32[8]{0:T(128)} %param.16) | copy-start | bytes 100
  11.8 18.7 %copy-start.3 = (bf16[8,128,128]{2,1,0:T(8,128)(2,1)S(1)}, bf16[8,128,128]{2,1,0:T(8,128)(2,1)}, u32[]{:S(2)}) copy-start(bf16[8,128,128]{2,1,0:T(8,128)(2,1)} %param.17) | copy-start | bytes 786436
  11.8 19.4 %copy-start.4 = (bf16[256,1024]{1,0:T(8,128)(2,1)S(1)}, bf16[256,1024]{1,0:T(8,128)(2,1)}, u32[]{:S(2)}) copy-start(bf16[256,1024]{1,0:T(8,128)(2,1)} %param.10) | copy-start | bytes 1572868
  11.8 32.8 %all-to-all-start = ((bf16[128,4,256]{2,1,0:T(4,128)(2,1)}), bf16[128,4,256]{2,1,0:T(4,128)(2,1)S(1)}, u32[]{:S(2)}, u32[]{:S(2)}) async-start(bf16[128,4,256]{2,1,0:T(4,128)(2,1)} %broadcast_select_fusion.1), calls=%async_computation | async-start | bytes 524288 | tf_op jit(solution)/shard_map/all_to_all | solution.py:23
  30.4 39.1 %reduce-scatter.2.cloned.1.call-start = ((), (), s32[]{:S(2)}) async-start(), calls=%async_computation.3 | async-start | bytes 1310720 | tf_op jit(solution)/shard_map/reduce_scatter | solution.py:43
  30.5 0.7 copy-start.9
  46.1 1.2 copy-start.2
  48.7 20.9 %copy-start.6 = (bf16[256,256]{1,0:T(8,128)(2,1)S(1)}, bf16[256,256]{1,0:T(8,128)(2,1)}, u32[]{:S(2)}) copy-start(bf16[256,256]{1,0:T(8,128)(2,1)} %param.12) | copy-start | bytes 393220
  84.7 0.7 copy-start.12
  87.2 37.1 %all-to-all-start.1 = ((f32[128,4,256]{2,1,0:T(4,128)}), f32[128,4,256]{2,1,0:T(4,128)S(1)}, u32[]{:S(2)}, u32[]{:S(2)}) async-start(f32[128,4,256]{2,1,0:T(4,128)} %reshape.101), calls=%async_computation.2 | async-start | bytes 1048576 | tf_op jit(solution)/shard_map/all_to_all | solution.py:73
  104.8 204.1 %all-reduce.3.cloned.1.call-start = ((), (), s32[]{:S(2)}) async-start(), calls=%async_computation.4 | async-start | bytes 4194304 | tf_op jit(solution)/shard_map/psum | solution.py:58
  106.2 1.0 copy-start.5
  124.4 0.7 copy-start.8
Sparse Core Ops, SparseCore 0:
  48.8 20.6 reduce-scatter.1
  109.3 199.5 all-reduce.2
where the time goes:
time: 321 us; the launch traced here: 319 us
  waiting for transfers between devices  229 us (71%)
  starting transfers between devices  36.2 us (11%)
  between operations  14.4 us (4%)
  local copies, waits for them, and re-layouts  11 us (3%)
  blocking collectives  10.8 us (3%)
  other arithmetic  9.99 us (3%)
  matrix products  7.94 us (2%)
    psum x1, waiting for transfers between devices, local(): sum_self, sum_neigh = lax.psum((local_self, local_neigh), 'dom')  179 us
    reduce_scatter x1, waiting for transfers between devices, local(): lax.psum_scatter(partial_value, 'rep', scatter_dimension=1, tiled=True)  20.8 us
    all_to_all x1, starting transfers between devices, local(): lax.all_to_all(outgoing, 'dom', split_axis=0, concat_axis=0, tiled=True)  18.6 us
    all_to_all x1, starting transfers between devices, local(): lax.all_to_all(mirror_grad, 'dom', split_axis=0, concat_axis=0, tiled=True)  17.6 us
    all_to_all x1, waiting for transfers between devices, local(): lax.all_to_all(mirror_grad, 'dom', split_axis=0, concat_axis=0, tiled=True)  16.7 us
    all_to_all x1, waiting for transfers between devices, local(): lax.all_to_all(outgoing, 'dom', split_axis=0, concat_axis=0, tiled=True)  12.1 us
    all_gather x1, blocking collectives, local(): grad_full = lax.all_gather(grad_pre, 'rep', axis=1, tiled=True)  10.8 us
  transfers between devices with their start and end apart: 4, of which 4 were waited for; matrix products, arithmetic and copies ran while one was open for 3% of the time, Pallas kernels for 0%

commit v1 on v0

v1 whole, which is shorter than its diff:
```python
import functools

import jax
import jax.numpy as jnp
from jax import lax
from jax.experimental import pallas as pl
from jax.experimental.pallas import tpu as pltpu
from jax.sharding import PartitionSpec as P

MESH = pl.DeviceIdType.MESH
F32 = jnp.float32
BF16 = jnp.bfloat16
CORES = 2
GRIDS = {128: (8, 8), 8: (2, 2)}
CUTS = {8: (2, 4), 2: (1, 2)}

NN = (((1,), (0,)), ((), ()))
TN = (((0,), (0,)), ((), ()))
NT = (((1,), (1,)), ((), ()))


def dot(a, b, dims=NN):
    return lax.dot_general(a, b, dims, preferred_element_type=F32)


class Exchange:
    def __init__(self, n, me, device, src, dst, send_sem, recv_sem):
        self.n, self.me, self.device = n, me, device
        self.src, self.dst = src, dst
        self.send_sem, self.recv_sem = send_sem, recv_sem

    def copy(self, k, src, dst, peer):
        return pltpu.make_async_remote_copy(
            src_ref=src,
            dst_ref=dst,
            send_sem=self.send_sem.at[k - 1],
            recv_sem=self.recv_sem.at[k - 1],
            device_id=self.device(peer),
            device_id_type=MESH,
        )

    def each(self, step):
        if self.n == 2:
            step(1)
        else:
            lax.fori_loop(1, self.n, lambda k, c: (step(k), c)[1], 0)

    def outgoing(self, k):
        peer = lax.rem(self.me + k, self.n)
        return self.copy(k, self.src(peer), self.dst(self.me, k), peer)

    def start(self):
        self.each(lambda k: self.outgoing(k).start())

    def wait_send(self):
        self.each(lambda k: self.outgoing(k).wait_send())

    def wait_recv_one(self, k):
        peer = lax.rem(self.me - k + self.n, self.n)
        slot = self.dst(peer, k)
        self.copy(k, slot, slot, peer).wait_recv()

    def wait_recv(self):
        self.each(self.wait_recv_one)


def kernel(
    dims,
    feat, w_self, w_neigh, grad_out, list_t, count, tile_dst, tile_src, tiles,
    hidden, grad_feat, out_w,
    perm01, perm10, hot0, hot1, edges, degree, table,
    o0, a0, s0, b0, o1, a1, s1, b1,
    part, pre_send, pre_recv, grads, grads_peer, lhs, lhs_peer, direct,
    c0, d0, e0, f0, c1, d1, e1, f1,
    w_acc, wa_send, wa_recv, wb_send, wb_recv, wb_own,
    sem_a, sem_b, sem_c, sem_d, sem_e, sem_f, sem_g, sem_h,
    sem_i, sem_j, sem_k, sem_l, sem_m, sem_n, sem_o, sem_p, sem_q, sem_r, sem_s, sem_t, sem_u,
):
    ny, nz, nx = dims
    ng = nz * CORES
    nd = ny * ng
    rows, width = feat.shape
    half = width // 2
    slots = list_t.shape[0]
    entries = nd * slots
    tile_count, tile_rows = tiles.shape[0], tiles.shape[1]
    dst_count = rows // tile_rows
    src_count = (rows + entries) // tile_rows
    full = nx * width

    dom = lax.axis_index("dom")
    x = lax.axis_index("rep")
    y = lax.div(dom, ng)
    g = lax.rem(dom, ng)
    z = lax.div(g, CORES)
    c = lax.rem(g, CORES)

    def at_g(peer):
        return (y * ng + peer, x)

    def at_y(peer):
        return (peer * ng + g, x)

    def at_z(peer):
        return (y * ng + peer * CORES + c, x)

    def at_c(peer):
        return (y * ng + z * CORES + peer, x)

    def at_x(peer):
        return (dom, peer)

    barrier = pltpu.get_barrier_semaphore()

    def greet(n, me, device):
        def step(k, carry):
            pl.semaphore_signal(
                barrier, inc=1, device_id=device(lax.rem(me + k, n)), device_id_type=MESH
            )
            return carry

        lax.fori_loop(1, n, step, 0)

    greet(ng, g, at_g)
    greet(ny, y, at_y)
    greet(nx, x, at_x)

    def iota(shape, axis):
        return lax.broadcasted_iota(jnp.int32, shape, axis)

    col = iota((1, entries), 1)
    row = iota((entries, entries), 0)

    def selection(index):
        return jnp.where(row == index, 1.0, 0.0).astype(BF16)

    from_listed = selection(lax.rem(col, slots) * nd + lax.div(col, slots))
    y_in = lax.rem(lax.div(col, slots), ny)
    g_in = lax.div(col, slots * ny)
    slot_in = lax.rem(col, slots)
    perm01[...] = selection((y_in * ng + g_in) * slots + slot_in)

    listed = jnp.concatenate(
        [jnp.where(j < count[...], list_t[j : j + 1, :], -1) for j in range(slots)], axis=1
    )
    listed = jnp.broadcast_to(listed.astype(F32), (8, entries)).astype(BF16)
    natural = dot(listed, from_listed)
    transposed = dot(natural.astype(BF16), perm01[...])
    vertex = iota((rows, entries), 0).astype(F32)
    hot0[...] = jnp.where(vertex == transposed[0:1, :], 1.0, 0.0).astype(BF16)
    hot1[...] = jnp.where(vertex == natural[0:1, :], 1.0, 0.0).astype(BF16)
    per_g, per_y = entries // ng, entries // ny
    o0[...] = dot(hot0[...], feat[:, :half], TN).astype(BF16).reshape(ng, per_g, half)
    o1[...] = dot(hot1[...], feat[:, half:], TN).astype(BF16).reshape(ny, per_y, half)

    pl.semaphore_wait(barrier, (ng - 1) + (ny - 1) + (nx - 1))

    out_a0 = Exchange(ng, g, at_g, lambda p: o0.at[p], lambda s, k: a0.at[s], *sem_pair(sem_a))
    out_a1 = Exchange(ny, y, at_y, lambda p: o1.at[p], lambda s, k: a1.at[s], *sem_pair(sem_b))
    out_b0 = Exchange(ny, y, at_y, lambda p: s0.at[p], lambda s, k: b0.at[s], *sem_pair(sem_c))
    out_b1 = Exchange(ng, g, at_g, lambda p: s1.at[p], lambda s, k: b1.at[s], *sem_pair(sem_d))
    out_a0.start()
    out_a1.start()
    a0[g] = o0[g]
    a1[y] = o1[y]

    y_out = lax.div(col, slots * ng)
    g_out = lax.rem(lax.div(col, slots), ng)
    perm10[...] = selection((g_out * ny + y_out) * slots + slot_in)
    table[:rows, :] = feat[...]
    lhs[0] = feat[...]
    part[...] = dot(feat[...], w_self[...])
    block_of = tile_dst[...] * src_count + tile_src[...]
    for d in range(dst_count):
        for s in range(src_count):
            here = jnp.where(block_of == d * src_count + s, 1.0, 0.0)
            total = jnp.zeros((tile_rows, tile_rows), F32)
            for t in range(tile_count):
                total += here[:, t : t + 1] * tiles[t].astype(F32)
            top = total.astype(BF16)
            at = (pl.ds(d * tile_rows, tile_rows), pl.ds(s * tile_rows, tile_rows))
            edges[(0,) + at] = top
            edges[(1,) + at] = (total - top.astype(F32)).astype(BF16)
    ones = jnp.ones((rows + entries, tile_rows), BF16)
    degree[...] = jnp.maximum(dot(edges[0], ones) + dot(edges[1], ones), 1.0)

    out_a0.wait_recv()
    s0[...] = dot(perm01[...], a0[...].reshape(entries, half)).astype(BF16).reshape(ny, per_y, half)
    out_b0.start()
    out_a1.wait_recv()
    s1[...] = dot(perm10[...], a1[...].reshape(entries, half)).astype(BF16).reshape(ng, per_g, half)
    out_b1.start()
    b0[y] = s0[y]
    b1[g] = s1[g]
    out_b0.wait_recv()
    table[rows:, :half] = b0[...].reshape(entries, half)
    out_b1.wait_recv()
    table[rows:, half:] = dot(perm01[...], b1[...].reshape(entries, half)).astype(BF16)

    safe = jnp.concatenate([degree[...]] * (width // tile_rows), axis=1)
    summed = dot(edges[0], table[...]) + dot(edges[1], table[...])
    lhs[1] = (summed / safe).astype(BF16)

    send_lhs = Exchange(
        CORES, c, at_c, lambda p: lhs.at[p], lambda s, k: lhs_peer, *sem_pair(sem_e)
    )
    send_lhs.start()

    for q in range(nx):
        here = pl.ds(q * width, width)
        part[:, here] += dot(lhs[1], w_neigh[:, here])
        pre_send[q] = part[:, here].astype(BF16)
    pre = Exchange(
        nx, x, at_x, lambda p: pre_send.at[p], lambda s, k: pre_recv.at[k - 1], *sem_pair(sem_f)
    )
    pre.start()
    pre_act = part[:, pl.ds(pl.multiple_of(x * width, width), width)]
    pre.wait_recv()
    for k in range(nx - 1):
        pre_act = pre_act + pre_recv[k].astype(F32)
    sig = jax.nn.sigmoid(pre_act)
    hidden[...] = (pre_act * sig).astype(BF16)
    grads[x] = (grad_out[...].astype(F32) * (sig + pre_act * sig * (1.0 - sig))).astype(BF16)

    gather = Exchange(nx, x, at_x, lambda p: grads.at[x], lambda s, k: grads.at[s], *sem_pair(sem_g))
    gather.start()

    def pass_on(q, sem):
        return Exchange(
            CORES, c, at_c, lambda p: grads.at[q], lambda s, k: grads_peer.at[q], *sem_pair(sem)
        )

    passes = [pass_on(x, sem_h)] + [
        pass_on(lax.rem(x - k + nx, nx), sem)
        for k, sem in zip(range(1, nx), (sem_i, sem_j, sem_k))
    ]
    passes[0].start()
    for k in range(1, nx):
        gather.wait_recv_one(k)
        passes[k].start()

    direct[...] = jnp.zeros_like(direct)
    grad_agg = jnp.zeros((rows, width), F32)
    for q in range(nx):
        here = pl.ds(q * width, width)
        direct[...] += dot(grads[q], w_self[:, here], NT)
        grad_agg += dot(grads[q], w_neigh[:, here], NT)
    grad_agg = (grad_agg / safe).astype(BF16)
    table_grad = dot(edges[0], grad_agg, TN) + dot(edges[1], grad_agg, TN)
    direct[...] += table_grad[:rows, :]
    mirror = table_grad[rows:, :].astype(BF16)

    c0[...] = mirror[:, :half].reshape(ny, per_y, half)
    c1[...] = dot(perm10[...], mirror[:, half:]).astype(BF16).reshape(ng, per_g, half)
    back_d0 = Exchange(ny, y, at_y, lambda p: c0.at[p], lambda s, k: d0.at[s], *sem_pair(sem_l))
    back_d1 = Exchange(ng, g, at_g, lambda p: c1.at[p], lambda s, k: d1.at[s], *sem_pair(sem_m))
    back_f0 = Exchange(ng, g, at_g, lambda p: e0.at[p], lambda s, k: f0.at[s], *sem_pair(sem_n))
    back_f1 = Exchange(ny, y, at_y, lambda p: e1.at[p], lambda s, k: f1.at[s], *sem_pair(sem_o))
    back_d0.start()
    back_d1.start()
    d0[y] = c0[y]
    d1[g] = c1[g]

    w_half = full // 2
    ry, rz = width // ny, width // nz
    send_lhs.wait_recv()
    for p in passes:
        p.wait_recv()
    own = lhs[c]
    other = lhs_peer[...]
    for q in range(nx):
        here = pl.ds(q * width, width)
        block = dot(own, grads[q], TN) + dot(other, grads_peer[q], TN)
        w_acc[:, here] = block
        h, at = divmod(q * width, w_half)
        block = block.astype(BF16)
        if h == 0:
            wa_send[0, :, :, pl.ds(at, width)] = block.reshape(ny, ry, width)
        else:
            wa_send[1, :, :, pl.ds(at, width)] = block.reshape(nz, rz, width)

    ways = (
        dict(n=ny, me=y, at=at_y, rows=ry, sem=sem_p),
        dict(n=nz, me=z, at=at_z, rows=rz, sem=sem_q),
    )

    def first(h):
        way = ways[h]
        return Exchange(
            way["n"], way["me"], way["at"],
            lambda p: wa_send.at[h, p], lambda s, k: wa_recv.at[h, k - 1], *sem_pair(way["sem"])
        )

    firsts = [first(0), first(1)]
    for way in firsts:
        way.start()

    back_d0.wait_recv()
    e0[...] = dot(perm10[...], d0[...].reshape(entries, half)).astype(BF16).reshape(ng, per_g, half)
    back_f0.start()
    back_d1.wait_recv()
    e1[...] = dot(perm01[...], d1[...].reshape(entries, half)).astype(BF16).reshape(ny, per_y, half)
    back_f1.start()
    f0[g] = e0[g]
    f1[y] = e1[y]

    def second(h):
        way = ways[1 - h]
        return Exchange(
            way["n"], way["me"], way["at"],
            lambda p: wb_send.at[h, p], lambda s, k: wb_recv.at[h, k - 1],
            *sem_pair((sem_r, sem_s)[h])
        )

    seconds = [second(0), second(1)]
    for h in range(2):
        firsts[h].wait_recv()
        way, after = ways[h], ways[1 - h]
        own_rows = pl.ds(pl.multiple_of(way["me"] * way["rows"], way["rows"]), way["rows"])
        total = w_acc[own_rows, pl.ds(h * w_half, w_half)]
        for k in range(way["n"] - 1):
            total = total + wa_recv[h, k].astype(F32)
        cut_rows, cut_cols = CUTS[after["n"]]
        tr, tc = way["rows"] // cut_rows, w_half // cut_cols
        for i in range(after["n"]):
            r, q = divmod(i, cut_cols)
            piece = total[r * tr : (r + 1) * tr, q * tc : (q + 1) * tc]
            wb_own[h, i] = piece
            wb_send[h, i] = piece.astype(BF16)
        seconds[h].start()

    back_f0.wait_recv()
    grad_feat[:, :half] = (
        direct[:, :half] + dot(hot0[...], f0[...].reshape(entries, half))
    ).astype(BF16)
    back_f1.wait_recv()
    grad_feat[:, half:] = (
        direct[:, half:] + dot(hot1[...], f1[...].reshape(entries, half))
    ).astype(BF16)

    scale = float(rows * nd) ** (-0.5)

    def tile_at(h, i):
        way, after = ways[h], ways[1 - h]
        cut_rows, cut_cols = CUTS[after["n"]]
        tr, tc = way["rows"] // cut_rows, w_half // cut_cols
        r = way["me"] * way["rows"] + lax.div(i, cut_cols) * tr
        q = h * w_half + lax.rem(i, cut_cols) * tc
        return out_w.at[c, pl.ds(pl.multiple_of(r, tr), tr), pl.ds(pl.multiple_of(q, tc), tc)]

    def third(h):
        after = ways[1 - h]
        return Exchange(
            after["n"], after["me"], after["at"],
            lambda p: tile_at(h, after["me"]), lambda s, k: tile_at(h, s),
            *sem_pair((sem_t, sem_u)[h])
        )

    def rows_at(h, i):
        way = ways[h]
        r = pl.multiple_of(i * way["rows"], way["rows"])
        return out_w.at[c, pl.ds(r, way["rows"]), pl.ds(h * w_half, w_half)]

    def fourth(h):
        way = ways[h]
        return Exchange(
            way["n"], way["me"], way["at"],
            lambda p: rows_at(h, way["me"]), lambda s, k: rows_at(h, s),
            *sem_pair(way["sem"], 1)
        )

    thirds, fourths = [third(0), third(1)], [fourth(0), fourth(1)]
    for h in range(2):
        seconds[h].wait_recv()
        after = ways[1 - h]
        total = wb_own[h, after["me"]]
        for k in range(after["n"] - 1):
            total = total + wb_recv[h, k].astype(F32)
        tile_at(h, after["me"])[...] = (total * scale).astype(BF16)
        thirds[h].start()
    for h in range(2):
        thirds[h].wait_recv()
        fourths[h].start()
    for h in range(2):
        fourths[h].wait_recv()
    swap = Exchange(
        CORES, c, at_c, lambda p: out_w.at[c], lambda s, k: out_w.at[s], *sem_pair(sem_e, 1)
    )
    swap.start()
    swap.wait_recv()
    for done in (
        [out_a0, out_a1, out_b0, out_b1, send_lhs, pre, gather, back_d0, back_d1, back_f0, back_f1]
        + passes + firsts + seconds + thirds + fourths + [swap]
    ):
        done.wait_send()


def sem_pair(sems, use=0):
    return sems.at[use, 0], sems.at[use, 1]


def solution(mesh):
    doms, nx = mesh.shape["dom"], mesh.shape["rep"]
    ny, nz = GRIDS[doms]
    ng = nz * CORES

    def local(
        features, w_self, w_neigh, grad_out, mirror_list, mirror_count, tile_dst, tile_src, tiles
    ):
        rows, width = features.shape
        half, full = width // 2, width * nx
        slots = mirror_list.shape[1]
        entries = doms * slots
        tile_rows = tiles.shape[1]
        per_g, per_y = entries // ng, entries // ny
        w_half = full // 2
        assert ny == nz
        block = width // ny
        cut_rows, cut_cols = CUTS[nz]
        tr, tc = block // cut_rows, w_half // cut_cols
        vmem = pl.BlockSpec(memory_space=pltpu.VMEM)

        def scratch(*shape, kind=BF16):
            return pltpu.VMEM(shape, kind)

        def sems(n, uses=1):
            return pltpu.SemaphoreType.DMA((uses, 2, n - 1))

        by_g, by_y = scratch(ng, per_g, half), scratch(ny, per_y, half)
        buffers = [
            scratch(entries, entries), scratch(entries, entries),
            scratch(rows, entries), scratch(rows, entries),
            scratch(2, rows, rows + entries), scratch(rows, tile_rows, kind=F32),
            scratch(rows + entries, width),
            by_g, by_g, by_y, by_y, by_y, by_y, by_g, by_g,
            scratch(rows, full, kind=F32), scratch(nx, rows, width), scratch(nx - 1, rows, width),
            scratch(nx, rows, width), scratch(nx, rows, width),
            scratch(2, rows, width), scratch(rows, width), scratch(rows, width, kind=F32),
            by_y, by_y, by_g, by_g, by_g, by_g, by_y, by_y,
            scratch(width, full, kind=F32),
            scratch(2, ny, block, w_half), scratch(2, ny - 1, block, w_half),
            scratch(2, nz, tr, tc), scratch(2, nz - 1, tr, tc), scratch(2, nz, tr, tc, kind=F32),
        ]
        semaphores = [
            sems(ng), sems(ny), sems(ny), sems(ng),
            sems(2, 2), sems(nx), sems(nx),
            sems(2), sems(2), sems(2), sems(2),
            sems(ny), sems(ng), sems(ng), sems(ny),
            sems(ny, 2), sems(nz, 2), sems(nz), sems(ny), sems(nz), sems(ny),
        ]
        hidden, grad_feat, out_w = pl.pallas_call(
            functools.partial(kernel, (ny, nz, nx)),
            out_shape=(
                jax.ShapeDtypeStruct((rows, width), BF16),
                jax.ShapeDtypeStruct((rows, width), BF16),
                jax.ShapeDtypeStruct((2, width, full), BF16),
            ),
            in_specs=[vmem] * 9,
            out_specs=(vmem, vmem, vmem),
            scratch_shapes=buffers + semaphores,
            compiler_params=pltpu.CompilerParams(
                collective_id=0, has_side_effects=True, vmem_limit_bytes=40 * 2**20
            ),
        )(
            features, w_self, w_neigh, grad_out, mirror_list.T, mirror_count[None, :],
            tile_dst[None, :], tile_src[None, :], tiles,
        )
        return hidden, grad_feat, out_w[0], out_w[1]

    in_specs = (
        P("dom", "rep"),
        P("rep", None),
        P("rep", None),
        P("dom", "rep"),
        P("dom", None),
        P("dom"),
        P("dom"),
        P("dom"),
        P("dom", None, None),
    )
    out_specs = (P("dom", "rep"), P("dom", "rep"), P("rep", None), P("rep", None))
    return jax.shard_map(local, mesh=mesh, in_specs=in_specs, out_specs=out_specs, check_vma=False)
```

time: 321 us -> 90.9 us (0.28)
  waiting for transfers between devices: 229 us -> 0 us
  Pallas kernels: 0 us -> 82.1 us
  starting transfers between devices: 36.2 us -> 0 us
  between operations: 14.4 us -> 0.68 us
  blocking collectives: 10.8 us -> 0 us
  other arithmetic: 9.99 us -> 0 us
  matrix products: 7.94 us -> 0 us
    psum x1 -> x0, waiting for transfers between devices: 179 us -> none  [local(): sum_self, sum_neigh = lax.psum((local_self, local_neigh), 'dom')]
    pallas_call x0 -> x1, Pallas kernels: none -> 82.1 us  [local(): pl.pallas_call(functools.partial(kernel, (ny, nz, nx)), out_shape=(jax.Sh...]
    all_to_all x2 -> x0, starting transfers between devices: 36.1 us -> none  [the longest x1 18.6 us: local(): lax.all_to_all(outgoing, 'dom', split_axis=0, concat_axis=0, tiled=True)]
    all_to_all x2 -> x0, waiting for transfers between devices: 28.7 us -> none  [the longest x1 16.7 us: local(): lax.all_to_all(mirror_grad, 'dom', split_axis=0, concat_axis=0, tiled=True)]
    reduce_scatter x1 -> x0, waiting for transfers between devices: 20.8 us -> none  [local(): lax.psum_scatter(partial_value, 'rep', scatter_dimension=1, tiled=True)]
    all_gather x1 -> x0, blocking collectives: 10.8 us -> none  [local(): grad_full = lax.all_gather(grad_pre, 'rep', axis=1, tiled=True)]
    dot_general x11 -> x0, matrix products: 7.94 us -> none  [the longest x1 1.35 us: local(): lax.dot_general(aggregated, grad_full, contract_rows, preferred_element_t...]
    convert_element_type x4 -> x0, other arithmetic: 4.24 us -> none  [the longest x1 1.75 us: local(): out_neigh = (sum_neigh * grad_scale).astype(jnp.bfloat16)]
  transfers between devices with their start and end apart: 4 -> 0, of which waited for: 4 -> 0; matrix products, arithmetic and copies ran while one was open for 3% -> 0% of each run, Pallas kernels for 0% -> 0%
where the time goes in v1:
time: 90.9 us; the launch traced here: 90.6 us
  Pallas kernels  82.1 us (90%)
  local copies, waits for them, and re-layouts  7.85 us (9%)
    pallas_call x1, Pallas kernels, local(): pl.pallas_call(functools.partial(kernel, (ny, nz, nx)), out_shape=(jax.Sh...  82.1 us
    unnamed x20, local copies, waits for them, and re-layouts  6.82 us

profile of v1, /device:TPU:1, one launch (start us, length us, event | category | flops | bytes accessed | tf_op | source)
XLA Modules:
  0.0 90.6 jit_solution(2743040674056720794)
XLA Ops:
  0.6 0.0 copy-start.5
  0.6 0.0 copy-start.6
  0.7 0.0 copy-start.7
  0.7 0.0 copy-start.8
  0.7 0.6 copy-done.5
  1.3 0.0 copy-done.6
  1.3 0.0 copy-done.7
  1.3 0.0 copy-done.8
  1.3 0.0 copy-start
  1.3 1.0 %copy-done = bf16[256,1024]{1,0:T(8,128)(2,1)S(1)} copy-done((bf16[256,1024]{1,0:T(8,128)(2,1)S(1)}, bf16[256,1024]{1,0:T(8,128)(2,1)}, u32[]{:S(2)}) %copy-start) | copy-done | bytes 524312
  2.4 0.0 copy-start.1
  2.4 1.0 %copy-done.1 = bf16[256,1024]{1,0:T(8,128)(2,1)S(1)} copy-done((bf16[256,1024]{1,0:T(8,128)(2,1)S(1)}, bf16[256,1024]{1,0:T(8,128)(2,1)}, u32[]{:S(2)}) %copy-start.1) | copy-done | bytes 524312
  3.4 0.0 copy-start.2
  3.4 0.9 %copy-done.2 = bf16[8,128,128]{2,1,0:T(8,128)(2,1)S(1)} copy-done((bf16[8,128,128]{2,1,0:T(8,128)(2,1)S(1)}, bf16[8,128,128]{2,1,0:T(8,128)(2,1)}, u32[]{:S(2)}) %copy-start.2) | copy-done | bytes 262168
  4.4 0.0 copy-start.3
  4.4 0.9 copy-done.3
  5.3 0.0 copy-start.4
  5.3 0.9 copy-done.4
  6.2 82.1 %shard_map.120 = (bf16[256,256]{1,0:T(8,128)(2,1)S(1)}, bf16[256,256]{1,0:T(8,128)(2,1)S(1)}, bf16[2,256,1024]{2,1,0:T(8,128)(2,1)S(1)}) custom-call(bf16[256,256]{1,0:T(8,128)(2,1)S(1)} %copy-done.3, bf16[256,1024]{1,0:T(8,128)(2,1)S(1)} %copy-done, bf16[256,1024]{1,0:T(8,128)(2,1)S(1)} %copy-done.1, bf16[256,256]{1,0:T(8,128)(2,1)S(1)} %copy-done.4, ...), custom_call_target="tpu_custom_call" | custom-call | tf_op jit(solution)/shard_map/pallas_call | solution.py:451
  88.3 1.0 %slice_bitcast_fusion = (bf16[256,1024]{1,0:T(8,128)(2,1)}, bf16[256,1024]{1,0:T(8,128)(2,1)}) fusion(bf16[2,256,1024]{2,1,0:T(8,128)(2,1)S(1)} %get-tuple-element.9), kind=kLoop, calls=%fused_computation | loop fusion | bytes 2097152 | tf_op jit(solution)/shard_map/squeeze | solution.py:468
  89.3 0.7 copy.15
  90.0 0.7 copy.16
Async XLA Ops:
  0.6 0.7 copy-start.5
  0.6 0.7 copy-start.6
  0.7 0.7 copy-start.7
  0.7 0.7 copy-start.8
  1.3 1.0 %copy-start = (bf16[256,1024]{1,0:T(8,128)(2,1)S(1)}, bf16[256,1024]{1,0:T(8,128)(2,1)}, u32[]{:S(2)}) copy-start(bf16[256,1024]{1,0:T(8,128)(2,1)} %w_self.1) | copy-start | bytes 1572868
  2.4 1.0 %copy-start.1 = (bf16[256,1024]{1,0:T(8,128)(2,1)S(1)}, bf16[256,1024]{1,0:T(8,128)(2,1)}, u32[]{:S(2)}) copy-start(bf16[256,1024]{1,0:T(8,128)(2,1)} %w_neigh.1) | copy-start | bytes 1572868
  3.4 0.9 %copy-start.2 = (bf16[8,128,128]{2,1,0:T(8,128)(2,1)S(1)}, bf16[8,128,128]{2,1,0:T(8,128)(2,1)}, u32[]{:S(2)}) copy-start(bf16[8,128,128]{2,1,0:T(8,128)(2,1)} %tiles.1) | copy-start | bytes 786436
  4.4 0.9 copy-start.3
  5.3 0.9 copy-start.4

commit v2 on v1

v2 whole, which is shorter than its diff:
```python
import functools

import jax
import jax.numpy as jnp
from jax import lax
from jax.experimental import pallas as pl
from jax.experimental.pallas import tpu as pltpu
from jax.sharding import PartitionSpec as P

MESH = pl.DeviceIdType.MESH
F32 = jnp.float32
BF16 = jnp.bfloat16
CORES = 2
GRIDS = {128: (8, 8), 8: (2, 2)}

NN = (((1,), (0,)), ((), ()))
TN = (((0,), (0,)), ((), ()))
NT = (((1,), (1,)), ((), ()))


def dot(a, b, dims=NN):
    return lax.dot_general(a, b, dims, preferred_element_type=F32)


class Exchange:
    def __init__(self, n, me, device, src, dst, send_sem, recv_sem):
        self.n, self.me, self.device = n, me, device
        self.src, self.dst = src, dst
        self.send_sem, self.recv_sem = send_sem, recv_sem

    def copy(self, k, src, dst, peer):
        return pltpu.make_async_remote_copy(
            src_ref=src,
            dst_ref=dst,
            send_sem=self.send_sem.at[k - 1],
            recv_sem=self.recv_sem.at[k - 1],
            device_id=self.device(peer),
            device_id_type=MESH,
        )

    def each(self, step):
        if self.n == 2:
            step(1)
        else:
            lax.fori_loop(1, self.n, lambda k, c: (step(k), c)[1], 0)

    def outgoing(self, k):
        peer = lax.rem(self.me + k, self.n)
        return self.copy(k, self.src(peer), self.dst(self.me, k), peer)

    def start(self):
        self.each(lambda k: self.outgoing(k).start())

    def wait_send(self):
        self.each(lambda k: self.outgoing(k).wait_send())

    def wait_recv_one(self, k):
        peer = lax.rem(self.me - k + self.n, self.n)
        slot = self.dst(peer, k)
        self.copy(k, slot, slot, peer).wait_recv()

    def wait_recv(self):
        self.each(self.wait_recv_one)


def kernel(
    dims,
    feat_in, w_self_in, w_neigh_in, grad_out_in, list_in, count_in, dst_in, src_in, tiles_in,
    hidden, grad_feat, out_w,
    weights, grad_out, list_t, count, tile_dst, tile_src, tiles,
    perm01, perm10, hot0, hot1, edges, degree, table,
    o0, a0, s0, b0, o1, a1, s1, b1,
    acts, acts_peer, w_cols, pre_act, grads, grads_peer, direct, grad_agg,
    c0, d0, e0, f0, c1, d1, e1, f1,
    w_acc, wa_send, wa_recv, wb_send, wb_recv, wt_send,
    in_sem,
    sem_a0, sem_a1, sem_b0, sem_b1, sem_feat, sem_cols, sem_cols_core, sem_agg, sem_acts,
    sem_gather, sem_pass, sem_d0, sem_d1, sem_f0, sem_f1, sem_first, sem_second,
    sem_third, sem_fourth, sem_swap,
):
    ny, nz, nx = dims
    ng = nz * CORES
    nd = ny * ng
    rows, width = feat_in.shape
    half = width // 2
    slots = list_in.shape[0]
    entries = nd * slots
    tile_count, tile_rows = tiles_in.shape[0], tiles_in.shape[1]
    dst_count = rows // tile_rows
    src_count = (rows + entries) // tile_rows
    parts = nz // nx
    band, piece = half // ny, width // parts

    dom = lax.axis_index("dom")
    x = lax.axis_index("rep")
    y = lax.div(dom, ng)
    g = lax.rem(dom, ng)
    z = lax.div(g, CORES)
    c = lax.rem(g, CORES)

    def at_g(peer):
        return (y * ng + peer, x)

    def at_y(peer):
        return (peer * ng + g, x)

    def at_z(peer):
        return (y * ng + peer * CORES + c, x)

    def at_c(peer):
        return (y * ng + z * CORES + peer, x)

    def at_x(peer):
        return (dom, peer)

    def fetch(i, src, dst):
        return pltpu.make_async_copy(src, dst, in_sem.at[i])

    fetches = [
        fetch(0, list_in, list_t),
        fetch(1, count_in, count),
        fetch(2, feat_in, acts.at[0, x]),
        fetch(3, w_self_in, weights.at[0]),
        fetch(4, w_neigh_in, weights.at[1]),
        fetch(5, dst_in, tile_dst),
        fetch(6, src_in, tile_src),
        fetch(7, tiles_in, tiles),
        fetch(8, grad_out_in, grad_out),
    ]
    for f in fetches:
        f.start()

    barrier = pltpu.get_barrier_semaphore()

    def greet_one(device):
        pl.semaphore_signal(barrier, inc=1, device_id=device, device_id_type=MESH)

    def greet(n, me, device):
        def step(k, carry):
            greet_one(device(lax.rem(me + k, n)))
            return carry

        lax.fori_loop(1, n, step, 0)

    greet(ng, g, at_g)
    greet(ny, y, at_y)
    greet(nx, x, at_x)

    ways = (dict(n=ny, me=y, at=at_y), dict(n=nz, me=z, at=at_z))

    def across(h, i, column):
        return (ways[1 - h]["at"](i)[0], column)

    def senders(h, step):
        def one(k, carry):
            i, column = x * parts + lax.div(k, nx), lax.rem(k, nx)

            @pl.when(jnp.logical_or(i != ways[1 - h]["me"], column != x))
            def _():
                step(k, i, column)

            return carry

        lax.fori_loop(0, parts * nx, one, 0)

    expected = (ng - 1) + (ny - 1) + (nx - 1)
    for h in range(2):
        senders(h, lambda k, i, column: greet_one(across(h, i, column)))
        after = ways[1 - h]
        mine = (lax.div(after["me"], parts) == x).astype(jnp.int32)
        expected = expected + after["n"] - mine

    def iota(shape, axis):
        return lax.broadcasted_iota(jnp.int32, shape, axis)

    col = iota((1, entries), 1)
    row = iota((entries, entries), 0)

    def selection(index):
        return jnp.where(row == index, 1.0, 0.0).astype(BF16)

    from_listed = selection(lax.rem(col, slots) * nd + lax.div(col, slots))
    y_in = lax.rem(lax.div(col, slots), ny)
    g_in = lax.div(col, slots * ny)
    slot_in = lax.rem(col, slots)
    perm01[...] = selection((y_in * ng + g_in) * slots + slot_in)

    fetches[0].wait()
    fetches[1].wait()
    listed = jnp.concatenate(
        [jnp.where(j < count[...], list_t[j : j + 1, :], -1) for j in range(slots)], axis=1
    )
    listed = jnp.broadcast_to(listed.astype(F32), (8, entries)).astype(BF16)
    natural = dot(listed, from_listed)
    transposed = dot(natural.astype(BF16), perm01[...])
    vertex = iota((rows, entries), 0).astype(F32)
    hot0[...] = jnp.where(vertex == transposed[0:1, :], 1.0, 0.0).astype(BF16)
    hot1[...] = jnp.where(vertex == natural[0:1, :], 1.0, 0.0).astype(BF16)
    per_g, per_y = entries // ng, entries // ny
    fetches[2].wait()
    feat = acts[0, x]
    o0[...] = dot(hot0[...], feat[:, :half], TN).astype(BF16).reshape(ng, per_g, half)
    o1[...] = dot(hot1[...], feat[:, half:], TN).astype(BF16).reshape(ny, per_y, half)

    pl.semaphore_wait(barrier, expected)

    out_a0 = Exchange(ng, g, at_g, lambda p: o0.at[p], lambda s, k: a0.at[s], *sem_pair(sem_a0))
    out_a1 = Exchange(ny, y, at_y, lambda p: o1.at[p], lambda s, k: a1.at[s], *sem_pair(sem_a1))
    out_b0 = Exchange(ny, y, at_y, lambda p: s0.at[p], lambda s, k: b0.at[s], *sem_pair(sem_b0))
    out_b1 = Exchange(ng, g, at_g, lambda p: s1.at[p], lambda s, k: b1.at[s], *sem_pair(sem_b1))
    out_a0.start()
    out_a1.start()

    def columns(p):
        return pl.ds(pl.multiple_of(p * width, width), width)

    feats = Exchange(
        nx, x, at_x, lambda p: acts.at[0, x], lambda s, k: acts.at[0, s], *sem_pair(sem_feat)
    )
    cols = Exchange(
        nx, x, at_x, lambda p: weights.at[c, :, columns(p)], lambda s, k: w_cols.at[c, s],
        *sem_pair(sem_cols)
    )
    cols_core = Exchange(
        CORES, c, at_c, lambda p: w_cols.at[c], lambda s, k: w_cols.at[s], *sem_pair(sem_cols_core)
    )
    fetches[3].wait()
    fetches[4].wait()
    cols.start()
    feats.start()
    a0[g] = o0[g]
    a1[y] = o1[y]
    w_cols[c, x] = weights[c, :, columns(x)]
    table[:rows, :] = feat

    y_out = lax.div(col, slots * ng)
    g_out = lax.rem(lax.div(col, slots), ng)
    perm10[...] = selection((g_out * ny + y_out) * slots + slot_in)
    for f in fetches[5:]:
        f.wait()

    out_a0.wait_recv()
    s0[...] = dot(perm01[...], a0[...].reshape(entries, half)).astype(BF16).reshape(ny, per_y, half)
    out_b0.start()
    out_a1.wait_recv()
    s1[...] = dot(perm10[...], a1[...].reshape(entries, half)).astype(BF16).reshape(ng, per_g, half)
    out_b1.start()
    b0[y] = s0[y]
    b1[g] = s1[g]

    block_of = tile_dst[...] * src_count + tile_src[...]
    for i in range(dst_count):
        for j in range(src_count):
            here = jnp.where(block_of == i * src_count + j, 1.0, 0.0)
            total = jnp.zeros((tile_rows, tile_rows), F32)
            for t in range(tile_count):
                total += here[:, t : t + 1] * tiles[t].astype(F32)
            top = total.astype(BF16)
            at = (pl.ds(i * tile_rows, tile_rows), pl.ds(j * tile_rows, tile_rows))
            edges[(0,) + at] = top
            edges[(1,) + at] = (total - top.astype(F32)).astype(BF16)
    ones = jnp.ones((rows + entries, tile_rows), BF16)
    degree[...] = jnp.maximum(dot(edges[0], ones) + dot(edges[1], ones), 1.0)
    cols.wait_recv()
    cols_core.start()

    out_b0.wait_recv()
    table[rows:, :half] = b0[...].reshape(entries, half)
    out_b1.wait_recv()
    table[rows:, half:] = dot(perm01[...], b1[...].reshape(entries, half)).astype(BF16)

    safe = jnp.concatenate([degree[...]] * (width // tile_rows), axis=1)
    summed = dot(edges[0], table[...]) + dot(edges[1], table[...])
    acts[1, x] = (summed / safe).astype(BF16)
    aggs = Exchange(
        nx, x, at_x, lambda p: acts.at[1, x], lambda s, k: acts.at[1, s], *sem_pair(sem_agg)
    )
    aggs.start()

    feats.wait_recv()
    cols_core.wait_recv()
    total = dot(acts[1, x], w_cols[1, x])
    for q in range(nx):
        total += dot(acts[0, q], w_cols[0, q])
    pre_act[...] = total
    for k in range(1, nx):
        q = lax.rem(x - k + nx, nx)
        aggs.wait_recv_one(k)
        pre_act[...] += dot(acts[1, q], w_cols[1, q])
    send_acts = Exchange(
        CORES, c, at_c, lambda p: acts.at[p], lambda s, k: acts_peer, *sem_pair(sem_acts)
    )
    send_acts.start()
    value = pre_act[...]
    sig = jax.nn.sigmoid(value)
    grads[x] = (grad_out[...].astype(F32) * (sig + value * sig * (1.0 - sig))).astype(BF16)

    send_grads = Exchange(
        CORES, c, at_c, lambda p: grads.at[x], lambda s, k: grads_peer, *sem_pair(sem_pass)
    )
    gather = Exchange(
        nx, x, at_x, lambda p: grads.at[x], lambda s, k: grads.at[s], *sem_pair(sem_gather)
    )
    send_grads.start()
    gather.start()
    hidden[...] = (value * sig).astype(BF16)

    for q in range(nx):
        w_acc[q] = dot(acts[c, q], grads[x], TN)
    send_acts.wait_recv()
    send_grads.wait_recv()
    for q in range(nx):
        block = w_acc[q] + dot(acts_peer[q], grads_peer[...], TN)
        w_acc[q] = block
        block = block.astype(BF16)
        for h in range(2):
            wa_send[h, :, q] = block[h * half : (h + 1) * half, :].reshape(ny, band, width)

    def first(h):
        way = ways[h]
        return Exchange(
            way["n"], way["me"], way["at"], lambda p: wa_send.at[h, p],
            lambda s, k: wa_recv.at[h, k - 1], *sem_pair(sem_first, h)
        )

    firsts = [first(0), first(1)]
    for way in firsts:
        way.start()

    direct[...] = dot(grads[x], weights[0, :, columns(x)], NT)
    grad_agg[...] = dot(grads[x], weights[1, :, columns(x)], NT)
    for k in range(1, nx):
        q = lax.rem(x - k + nx, nx)
        gather.wait_recv_one(k)
        direct[...] += dot(grads[q], weights[0, :, columns(q)], NT)
        grad_agg[...] += dot(grads[q], weights[1, :, columns(q)], NT)
    scaled = (grad_agg[...] / safe).astype(BF16)
    table_grad = dot(edges[0], scaled, TN) + dot(edges[1], scaled, TN)
    direct[...] += table_grad[:rows, :]
    mirror = table_grad[rows:, :].astype(BF16)

    c0[...] = mirror[:, :half].reshape(ny, per_y, half)
    c1[...] = dot(perm10[...], mirror[:, half:]).astype(BF16).reshape(ng, per_g, half)
    back_d0 = Exchange(ny, y, at_y, lambda p: c0.at[p], lambda s, k: d0.at[s], *sem_pair(sem_d0))
    back_d1 = Exchange(ng, g, at_g, lambda p: c1.at[p], lambda s, k: d1.at[s], *sem_pair(sem_d1))
    back_f0 = Exchange(ng, g, at_g, lambda p: e0.at[p], lambda s, k: f0.at[s], *sem_pair(sem_f0))
    back_f1 = Exchange(ny, y, at_y, lambda p: e1.at[p], lambda s, k: f1.at[s], *sem_pair(sem_f1))
    back_d0.start()
    back_d1.start()
    d0[y] = c0[y]
    d1[g] = c1[g]

    def second(h):
        way = ways[1 - h]
        return Exchange(
            way["n"], way["me"], way["at"], lambda p: wb_send.at[h, p],
            lambda s, k: wb_recv.at[h, k - 1], *sem_pair(sem_second, h)
        )

    seconds = [second(0), second(1)]
    for h in range(2):
        firsts[h].wait_recv()
        way, after = ways[h], ways[1 - h]
        own_rows = pl.ds(pl.multiple_of(h * half + way["me"] * band, band), band)
        for q in range(nx):
            total = w_acc[q, own_rows, :]
            for k in range(way["n"] - 1):
                total = total + wa_recv[h, k, q].astype(F32)
            for i in range(parts):
                wb_send[h, q * parts + i] = total[:, i * piece : (i + 1) * piece]
        seconds[h].start()

    back_d0.wait_recv()
    e0[...] = dot(perm10[...], d0[...].reshape(entries, half)).astype(BF16).reshape(ng, per_g, half)
    back_f0.start()
    back_d1.wait_recv()
    e1[...] = dot(perm01[...], d1[...].reshape(entries, half)).astype(BF16).reshape(ny, per_y, half)
    back_f1.start()
    f0[g] = e0[g]
    f1[y] = e1[y]

    scale = float(rows * nd) ** (-0.5)

    def piece_at(h, i, column):
        r = h * half + ways[h]["me"] * band
        q = column * width + lax.rem(i, parts) * piece
        return out_w.at[c, pl.ds(pl.multiple_of(r, band), band), pl.ds(pl.multiple_of(q, piece), piece)]

    def third(h, k, dst, device, slot):
        return pltpu.make_async_remote_copy(
            src_ref=wt_send.at[h], dst_ref=dst, send_sem=sem_third.at[h, 0, k],
            recv_sem=sem_third.at[h, 1, slot], device_id=device, device_id_type=MESH,
        )

    def thirds(h, step):
        after = ways[1 - h]
        me = after["me"]
        slot = lax.rem(me, parts) * nx + x
        target = lax.div(me, parts)

        def one(k, carry):
            copy = third(h, k, piece_at(h, me, x), across(h, lax.rem(me + k, after["n"]), target), slot)

            @pl.when(jnp.logical_or(k != 0, target != x))
            def _():
                step(copy)

            return carry

        lax.fori_loop(0, after["n"], one, 0)

    for h in range(2):
        seconds[h].wait_recv()
        after = ways[1 - h]
        total = wb_send[h, after["me"]]
        for k in range(after["n"] - 1):
            total = total + wb_recv[h, k]
        wt_send[h] = (total * scale).astype(BF16)
        thirds(h, lambda copy: copy.start())

        @pl.when(lax.div(after["me"], parts) == x)
        def _():
            piece_at(h, after["me"], x)[...] = wt_send[h]

    def band_at(h, i, core):
        return out_w.at[core, pl.ds(pl.multiple_of(h * half + i * band, band), band), :]

    def fourth(h):
        way = ways[h]
        return Exchange(
            way["n"], way["me"], way["at"], lambda p: band_at(h, way["me"], c),
            lambda s, k: band_at(h, s, c), *sem_pair(sem_fourth, h)
        )

    def swap(h, k):
        way = ways[h]
        i = lax.rem(way["me"] - k + way["n"], way["n"])
        return pltpu.make_async_remote_copy(
            src_ref=band_at(h, i, c), dst_ref=band_at(h, i, c), send_sem=sem_swap.at[h, 0, k],
            recv_sem=sem_swap.at[h, 1, k], device_id=at_c(1 - c), device_id_type=MESH,
        )

    fourths = [fourth(0), fourth(1)]
    for h in range(2):
        senders(
            h,
            lambda k, i, column: third(h, 0, piece_at(h, i, column), across(h, i, column), k).wait_recv(),
        )
        fourths[h].start()
        swap(h, 0).start()

    back_f0.wait_recv()
    grad_feat[:, :half] = (
        direct[:, :half] + dot(hot0[...], f0[...].reshape(entries, half))
    ).astype(BF16)
    back_f1.wait_recv()
    grad_feat[:, half:] = (
        direct[:, half:] + dot(hot1[...], f1[...].reshape(entries, half))
    ).astype(BF16)

    def pass_on(k):
        for h in range(2):
            fourths[h].wait_recv_one(k)
            swap(h, k).start()

    fourths[0].each(pass_on)

    def swapped(k, carry):
        for h in range(2):
            swap(h, k).wait_recv()
            swap(h, k).wait_send()
        return carry

    lax.fori_loop(0, ny, swapped, 0)
    for h in range(2):
        thirds(h, lambda copy: copy.wait_send())
    for done in (
        [out_a0, out_a1, out_b0, out_b1, feats, cols, cols_core, aggs, send_acts, send_grads]
        + [gather, back_d0, back_d1, back_f0, back_f1] + firsts + seconds + fourths
    ):
        done.wait_send()


def write_out(hidden, grad_feat, both, out0, out1, out2, out3, sem):
    pairs = ((hidden, out0), (grad_feat, out1), (both.at[0], out2), (both.at[1], out3))
    copies = [pltpu.make_async_copy(src, dst, sem.at[i]) for i, (src, dst) in enumerate(pairs)]
    for copy in copies:
        copy.start()
    for copy in copies:
        copy.wait()


def sem_pair(sems, use=0):
    return sems.at[use, 0], sems.at[use, 1]


def solution(mesh):
    doms, nx = mesh.shape["dom"], mesh.shape["rep"]
    ny, nz = GRIDS[doms]
    ng = nz * CORES

    def local(
        features, w_self, w_neigh, grad_out, mirror_list, mirror_count, tile_dst, tile_src, tiles
    ):
        rows, width = features.shape
        half, full = width // 2, width * nx
        slots = mirror_list.shape[1]
        entries = doms * slots
        tile_count, tile_rows = tiles.shape[0], tiles.shape[1]
        per_g, per_y = entries // ng, entries // ny
        assert ny == nz and rows == width and nz % nx == 0
        parts = nz // nx
        band, piece = half // ny, width // parts
        vmem, stay = (pl.BlockSpec(memory_space=s) for s in (pltpu.VMEM, pl.ANY))

        def scratch(*shape, kind=BF16):
            return pltpu.VMEM(shape, kind)

        def sems(n, uses=1):
            return pltpu.SemaphoreType.DMA((uses, 2, n))

        by_g, by_y = scratch(ng, per_g, half), scratch(ny, per_y, half)
        buffers = [
            scratch(2, width, full), scratch(rows, width),
            scratch(slots, doms, kind=jnp.int32), scratch(1, doms, kind=jnp.int32),
            scratch(1, tile_count, kind=jnp.int32), scratch(1, tile_count, kind=jnp.int32),
            scratch(tile_count, tile_rows, tile_rows),
            scratch(entries, entries), scratch(entries, entries),
            scratch(rows, entries), scratch(rows, entries),
            scratch(2, rows, rows + entries), scratch(rows, tile_rows, kind=F32),
            scratch(rows + entries, width),
            by_g, by_g, by_y, by_y, by_y, by_y, by_g, by_g,
            scratch(2, nx, rows, width), scratch(nx, rows, width), scratch(2, nx, width, width),
            scratch(rows, width, kind=F32), scratch(nx, rows, width), scratch(rows, width),
            scratch(rows, width, kind=F32), scratch(rows, width, kind=F32),
            by_y, by_y, by_g, by_g, by_g, by_g, by_y, by_y,
            scratch(nx, width, width, kind=F32),
            scratch(2, ny, nx, band, width), scratch(2, ny - 1, nx, band, width),
            scratch(2, nz, band, piece, kind=F32), scratch(2, nz - 1, band, piece, kind=F32),
            scratch(2, band, piece),
        ]
        semaphores = [
            pltpu.SemaphoreType.DMA((9,)),
            sems(ng - 1), sems(ny - 1), sems(ny - 1), sems(ng - 1),
            sems(nx - 1), sems(nx - 1), sems(1), sems(nx - 1), sems(1),
            sems(nx - 1), sems(1), sems(ny - 1), sems(ng - 1), sems(ng - 1), sems(ny - 1),
            sems(ny - 1, 2), sems(ny - 1, 2), sems(nz, 2), sems(ny - 1, 2), sems(ny, 2),
        ]
        shapes = (
            jax.ShapeDtypeStruct((rows, width), BF16),
            jax.ShapeDtypeStruct((rows, width), BF16),
            jax.ShapeDtypeStruct((2, width, full), BF16),
        )
        results = pl.pallas_call(
            functools.partial(kernel, (ny, nz, nx)),
            out_shape=shapes,
            in_specs=[pl.BlockSpec(memory_space=pltpu.HBM)] * 9,
            out_specs=(vmem, vmem, vmem),
            scratch_shapes=buffers + semaphores,
            compiler_params=pltpu.CompilerParams(
                collective_id=0, has_side_effects=True, vmem_limit_bytes=62 * 2**20
            ),
        )(
            features, w_self, w_neigh, grad_out, mirror_list.T, mirror_count[None, :],
            tile_dst[None, :], tile_src[None, :], tiles,
        )
        weight = jax.ShapeDtypeStruct((width, full), BF16)
        return pl.pallas_call(
            write_out,
            out_shape=shapes[:2] + (weight, weight),
            in_specs=[stay] * 3,
            out_specs=(stay,) * 4,
            scratch_shapes=[pltpu.SemaphoreType.DMA((4,))],
        )(*results)

    in_specs = (
        P("dom", "rep"),
        P("rep", None),
        P("rep", None),
        P("dom", "rep"),
        P("dom", None),
        P("dom"),
        P("dom"),
        P("dom"),
        P("dom", None, None),
    )
    out_specs = (P("dom", "rep"), P("dom", "rep"), P("rep", None), P("rep", None))
    return jax.shard_map(local, mesh=mesh, in_specs=in_specs, out_specs=out_specs, check_vma=False)
```

time: 90.9 us -> 118 us (1.30)
  Pallas kernels: 82.1 us -> 117 us
  local copies, waits for them, and re-layouts: 7.85 us -> 0 us
    pallas_call x1 -> x2, Pallas kernels: 82.1 us -> 117 us  [the longest x1 75.9 us: local(): pl.pallas_call(functools.partial(kernel, (ny, nz, nx)), out_shape=shapes,...]
    unnamed x20 -> x0, local copies, waits for them, and re-layouts: 6.82 us -> none
where the time goes in v2:
time: 118 us; the launch traced here: 117 us
  Pallas kernels  117 us (99%)
    pallas_call x1, Pallas kernels, local(): pl.pallas_call(functools.partial(kernel, (ny, nz, nx)), out_shape=shapes,...  75.9 us
    pallas_call x1, Pallas kernels, local(): pl.pallas_call(write_out, out_shape=shapes[:2] + (weight, weight), in_spe...  40.8 us

profile of v2, /device:TPU:1, one launch (start us, length us, event | category | flops | bytes accessed | tf_op | source)
XLA Modules:
  0.0 117.4 jit_solution(9511937400563439437)
XLA Ops:
  0.6 75.9 %shard_map.120 = (bf16[256,256]{1,0:T(8,128)(2,1)}, bf16[256,256]{1,0:T(8,128)(2,1)}, bf16[2,256,1024]{2,1,0:T(8,128)(2,1)}) custom-call(bf16[256,256]{1,0:T(8,128)(2,1)} %feat_in.1, bf16[256,1024]{1,0:T(8,128)(2,1)} %w_self_in.1, bf16[256,1024]{1,0:T(8,128)(2,1)} %w_neigh_in.1, bf16[256,256]{1,0:T(8,128)(2,1)} %grad_out_in.1, s32[4,128]{1,0:T(4,128)} %bitcast.4, ...), custom_call_target="tpu_custom_call" | custom-call | tf_op jit(solution)/shard_map/pallas_call | solution.py:554
  76.5 40.8 %shard_map.121 = (bf16[256,256]{1,0:T(8,128)(2,1)}, bf16[256,256]{1,0:T(8,128)(2,1)}, bf16[256,1024]{1,0:T(8,128)(2,1)}, bf16[256,1024]{1,0:T(8,128)(2,1)}) custom-call(bf16[256,256]{1,0:T(8,128)(2,1)} %get-tuple-element.7.hidden, bf16[256,256]{1,0:T(8,128)(2,1)} %get-tuple-element.8.grad_feat, bf16[2,256,1024]{2,1,0:T(8,128)(2,1)} %get-tuple-element.9.both), custom_call_target="tpu_custom_call" | custom-call | tf_op jit(solution)/shard_map/pallas_call | solution.py:568

commit v3 on v2

--- a/solution.py
+++ b/solution.py
@@ -553,25 +553,30 @@
         )
         results = pl.pallas_call(
             functools.partial(kernel, (ny, nz, nx)),
-            out_shape=shapes,
+            out_shape=tuple(pltpu.VMEM(v.shape, v.dtype) for v in shapes),
             in_specs=[pl.BlockSpec(memory_space=pltpu.HBM)] * 9,
             out_specs=(vmem, vmem, vmem),
             scratch_shapes=buffers + semaphores,
             compiler_params=pltpu.CompilerParams(
-                collective_id=0, has_side_effects=True, vmem_limit_bytes=62 * 2**20
+                collective_id=0, has_side_effects=True, vmem_limit_bytes=32 * 2**20
             ),
         )(
-            features, w_self, w_neigh, grad_out, mirror_list.T, mirror_count[None, :],
-            tile_dst[None, :], tile_src[None, :], tiles,
+            *(
+                pltpu.with_memory_space_constraint(v, pltpu.HBM)
+                for v in (
+                    features, w_self, w_neigh, grad_out, mirror_list.T, mirror_count[None, :],
+                    tile_dst[None, :], tile_src[None, :], tiles,
+                )
+            )
         )
         weight = jax.ShapeDtypeStruct((width, full), BF16)
         return pl.pallas_call(
             write_out,
             out_shape=shapes[:2] + (weight, weight),
-            in_specs=[stay] * 3,
+            in_specs=[vmem] * 3,
             out_specs=(stay,) * 4,
             scratch_shapes=[pltpu.SemaphoreType.DMA((4,))],
-        )(*results)
+        )(*(pltpu.with_memory_space_constraint(v, pltpu.VMEM) for v in results))
 
     in_specs = (
         P("dom", "rep"),

time: 118 us -> 77 us (0.65)
  Pallas kernels: 117 us -> 75.9 us
    pallas_call x1, Pallas kernels: 40.8 us -> 1.09 us  [local(): pl.pallas_call(write_out, out_shape=shapes[:2] + (weight, weight), in_spe...]
where the time goes in v3:
time: 77 us; the launch traced here: 76.6 us
  Pallas kernels  75.9 us (99%)
    pallas_call x1, Pallas kernels, local(): pl.pallas_call(functools.partial(kernel, (ny, nz, nx)), out_shape=tuple((...  74.9 us

profile of v3, /device:TPU:1, one launch (start us, length us, event | category | flops | bytes accessed | tf_op | source)
XLA Modules:
  0.0 76.6 jit_solution(18010412955603820126)
XLA Ops:
  0.6 74.9 %shard_map.120 = (bf16[256,256]{1,0:T(8,128)(2,1)S(1)}, bf16[256,256]{1,0:T(8,128)(2,1)S(1)}, bf16[2,256,1024]{2,1,0:T(8,128)(2,1)S(1)}) custom-call(bf16[256,256]{1,0:T(8,128)(2,1)} %feat_in.1, bf16[256,1024]{1,0:T(8,128)(2,1)} %w_self_in.1, bf16[256,1024]{1,0:T(8,128)(2,1)} %w_neigh_in.1, bf16[256,256]{1,0:T(8,128)(2,1)} %grad_out_in.1, s32[4,128]{1,0:T(4,128)} %bitcast.4, ...), custom_call_target="tpu_custom_call" | custom-call | tf_op jit(solution)/shard_map/pallas_call | solution.py:554
  75.5 1.1 %shard_map.121 = (bf16[256,256]{1,0:T(8,128)(2,1)}, bf16[256,256]{1,0:T(8,128)(2,1)}, bf16[256,1024]{1,0:T(8,128)(2,1)}, bf16[256,1024]{1,0:T(8,128)(2,1)}) custom-call(bf16[256,256]{1,0:T(8,128)(2,1)S(1)} %get-tuple-element.7.hidden, bf16[256,256]{1,0:T(8,128)(2,1)S(1)} %get-tuple-element.8.grad_feat, bf16[2,256,1024]{2,1,0:T(8,128)(2,1)S(1)} %get-tuple-element.9.both), custom_call_target="tpu_custom_call" | custom-call | tf_op jit(solution)/shard_map/pallas_call | solution.py:573

commit v4 on v3

--- a/solution.py
+++ b/solution.py
@@ -49,7 +49,16 @@
         return self.copy(k, self.src(peer), self.dst(self.me, k), peer)
 
     def start(self):
-        self.each(lambda k: self.outgoing(k).start())
+        if self.n == 2:
+            self.outgoing(1).start()
+            return
+
+        def step(j, carry):
+            k = self.n // 2 + lax.div(j + 1, 2) * (1 - 2 * lax.rem(j, 2))
+            self.outgoing(k).start()
+            return carry
+
+        lax.fori_loop(0, self.n - 1, step, 0)
 
     def wait_send(self):
         self.each(lambda k: self.outgoing(k).wait_send())
@@ -127,9 +136,6 @@
         fetch(7, tiles_in, tiles),
         fetch(8, grad_out_in, grad_out),
     ]
-    for f in fetches:
-        f.start()
-
     barrier = pltpu.get_barrier_semaphore()
 
     def greet_one(device):
@@ -169,6 +175,9 @@
         after = ways[1 - h]
         mine = (lax.div(after["me"], parts) == x).astype(jnp.int32)
         expected = expected + after["n"] - mine
+
+    for f in fetches:
+        f.start()
 
     def iota(shape, axis):
         return lax.broadcasted_iota(jnp.int32, shape, axis)
@@ -277,7 +286,16 @@
     )
     aggs.start()
 
+    def pass_acts(k):
+        q = lax.rem(x - k + nx, nx)
+        return Exchange(
+            CORES, c, at_c, lambda p: acts.at[p, q], lambda s, i: acts_peer.at[q],
+            *(sem.at[pl.ds(k, 1)] for sem in sem_pair(sem_acts))
+        )
+
     feats.wait_recv()
+    send_acts = [pass_acts(k) for k in range(nx)]
+    send_acts[0].start()
     cols_core.wait_recv()
     total = dot(acts[1, x], w_cols[1, x])
     for q in range(nx):
@@ -286,11 +304,8 @@
     for k in range(1, nx):
         q = lax.rem(x - k + nx, nx)
         aggs.wait_recv_one(k)
+        send_acts[k].start()
         pre_act[...] += dot(acts[1, q], w_cols[1, q])
-    send_acts = Exchange(
-        CORES, c, at_c, lambda p: acts.at[p], lambda s, k: acts_peer, *sem_pair(sem_acts)
-    )
-    send_acts.start()
     value = pre_act[...]
     sig = jax.nn.sigmoid(value)
     grads[x] = (grad_out[...].astype(F32) * (sig + value * sig * (1.0 - sig))).astype(BF16)
@@ -307,7 +322,8 @@
 
     for q in range(nx):
         w_acc[q] = dot(acts[c, q], grads[x], TN)
-    send_acts.wait_recv()
+    for done in send_acts:
+        done.wait_recv()
     send_grads.wait_recv()
     for q in range(nx):
         block = w_acc[q] + dot(acts_peer[q], grads_peer[...], TN)
@@ -370,6 +386,49 @@
                 wb_send[h, q * parts + i] = total[:, i * piece : (i + 1) * piece]
         seconds[h].start()
 
+    scale = float(rows * nd) ** (-0.5)
+
+    def piece_at(h, i, column):
+        r = h * half + ways[h]["me"] * band
+        q = column * width + lax.rem(i, parts) * piece
+        return out_w.at[c, pl.ds(pl.multiple_of(r, band), band), pl.ds(pl.multiple_of(q, piece), piece)]
+
+    def third(h, k, dst, device, slot):
+        return pltpu.make_async_remote_copy(
+            src_ref=wt_send.at[h], dst_ref=dst, send_sem=sem_third.at[h, 0, k],
+            recv_sem=sem_third.at[h, 1, slot], device_id=device, device_id_type=MESH,
+        )
+
+    def thirds(h, step):
+        after = ways[1 - h]
+        me = after["me"]
+        slot = lax.rem(me, parts) * nx + x
+        target = lax.div(me, parts)
+
+        def one(k, carry):
+            copy = third(h, k, piece_at(h, me, x), across(h, lax.rem(me + k, after["n"]), target), slot)
+
+            @pl.when(jnp.logical_or(k != 0, target != x))
+            def _():
+                step(copy)
+
+            return carry
+
+        lax.fori_loop(0, after["n"], one, 0)
+
+    for h in range(2):
+        seconds[h].wait_recv()
+        after = ways[1 - h]
+        total = wb_send[h, after["me"]]
+        for k in range(after["n"] - 1):
+            total = total + wb_recv[h, k]
+        wt_send[h] = (total * scale).astype(BF16)
+        thirds(h, lambda copy: copy.start())
+
+        @pl.when(lax.div(after["me"], parts) == x)
+        def _():
+            piece_at(h, after["me"], x)[...] = wt_send[h]
+
     back_d0.wait_recv()
     e0[...] = dot(perm10[...], d0[...].reshape(entries, half)).astype(BF16).reshape(ng, per_g, half)
     back_f0.start()
@@ -379,49 +438,6 @@
     f0[g] = e0[g]
     f1[y] = e1[y]
 
-    scale = float(rows * nd) ** (-0.5)
-
-    def piece_at(h, i, column):
-        r = h * half + ways[h]["me"] * band
-        q = column * width + lax.rem(i, parts) * piece
-        return out_w.at[c, pl.ds(pl.multiple_of(r, band), band), pl.ds(pl.multiple_of(q, piece), piece)]
-
-    def third(h, k, dst, device, slot):
-        return pltpu.make_async_remote_copy(
-            src_ref=wt_send.at[h], dst_ref=dst, send_sem=sem_third.at[h, 0, k],
-            recv_sem=sem_third.at[h, 1, slot], device_id=device, device_id_type=MESH,
-        )
-
-    def thirds(h, step):
-        after = ways[1 - h]
-        me = after["me"]
-        slot = lax.rem(me, parts) * nx + x
-        target = lax.div(me, parts)
-
-        def one(k, carry):
-            copy = third(h, k, piece_at(h, me, x), across(h, lax.rem(me + k, after["n"]), target), slot)
-
-            @pl.when(jnp.logical_or(k != 0, target != x))
-            def _():
-                step(copy)
-
-            return carry
-
-        lax.fori_loop(0, after["n"], one, 0)
-
-    for h in range(2):
-        seconds[h].wait_recv()
-        after = ways[1 - h]
-        total = wb_send[h, after["me"]]
-        for k in range(after["n"] - 1):
-            total = total + wb_recv[h, k]
-        wt_send[h] = (total * scale).astype(BF16)
-        thirds(h, lambda copy: copy.start())
-
-        @pl.when(lax.div(after["me"], parts) == x)
-        def _():
-            piece_at(h, after["me"], x)[...] = wt_send[h]
-
     def band_at(h, i, core):
         return out_w.at[core, pl.ds(pl.multiple_of(h * half + i * band, band), band), :]
 
@@ -475,8 +491,8 @@
     for h in range(2):
         thirds(h, lambda copy: copy.wait_send())
     for done in (
-        [out_a0, out_a1, out_b0, out_b1, feats, cols, cols_core, aggs, send_acts, send_grads]
-        + [gather, back_d0, back_d1, back_f0, back_f1] + firsts + seconds + fourths
+        [out_a0, out_a1, out_b0, out_b1, feats, cols, cols_core, aggs, send_grads]
+        + [gather, back_d0, back_d1, back_f0, back_f1] + send_acts + firsts + seconds + fourths
     ):
         done.wait_send()
 
@@ -542,7 +558,7 @@
         semaphores = [
             pltpu.SemaphoreType.DMA((9,)),
             sems(ng - 1), sems(ny - 1), sems(ny - 1), sems(ng - 1),
-            sems(nx - 1), sems(nx - 1), sems(1), sems(nx - 1), sems(1),
+            sems(nx - 1), sems(nx - 1), sems(1), sems(nx - 1), sems(nx),
             sems(nx - 1), sems(1), sems(ny - 1), sems(ng - 1), sems(ng - 1), sems(ny - 1),
             sems(ny - 1, 2), sems(ny - 1, 2), sems(nz, 2), sems(ny - 1, 2), sems(ny, 2),
         ]

time: 77 us -> 74.2 us (0.964)
  Pallas kernels: 75.9 us -> 73.4 us
    pallas_call x1, Pallas kernels: 74.9 us -> 72.3 us  [local(): pl.pallas_call(functools.partial(kernel, (ny, nz, nx)), out_shape=tuple((...]
where the time goes in v4:
time: 74.2 us; the launch traced here: 74 us
  Pallas kernels  73.4 us (99%)
    pallas_call x1, Pallas kernels, local(): pl.pallas_call(functools.partial(kernel, (ny, nz, nx)), out_shape=tuple((...  72.3 us

profile of v4, /device:TPU:1, one launch (start us, length us, event | category | flops | bytes accessed | tf_op | source)
XLA Modules:
  0.0 74.0 jit_solution(6872721442472464001)
XLA Ops:
  0.6 72.3 %shard_map.120 = (bf16[256,256]{1,0:T(8,128)(2,1)S(1)}, bf16[256,256]{1,0:T(8,128)(2,1)S(1)}, bf16[2,256,1024]{2,1,0:T(8,128)(2,1)S(1)}) custom-call(bf16[256,256]{1,0:T(8,128)(2,1)} %feat_in.1, bf16[256,1024]{1,0:T(8,128)(2,1)} %w_self_in.1, bf16[256,1024]{1,0:T(8,128)(2,1)} %w_neigh_in.1, bf16[256,256]{1,0:T(8,128)(2,1)} %grad_out_in.1, s32[4,128]{1,0:T(4,128)} %bitcast.4, ...), custom_call_target="tpu_custom_call" | custom-call | tf_op jit(solution)/shard_map/pallas_call | solution.py:570
  72.9 1.1 %shard_map.121 = (bf16[256,256]{1,0:T(8,128)(2,1)}, bf16[256,256]{1,0:T(8,128)(2,1)}, bf16[256,1024]{1,0:T(8,128)(2,1)}, bf16[256,1024]{1,0:T(8,128)(2,1)}) custom-call(bf16[256,256]{1,0:T(8,128)(2,1)S(1)} %get-tuple-element.7.hidden, bf16[256,256]{1,0:T(8,128)(2,1)S(1)} %get-tuple-element.8.grad_feat, bf16[2,256,1024]{2,1,0:T(8,128)(2,1)S(1)} %get-tuple-element.9.both), custom_call_target="tpu_custom_call" | custom-call | tf_op jit(solution)/shard_map/pallas_call | solution.py:589

commit v5 on v4

--- a/solution.py
+++ b/solution.py
@@ -81,11 +81,11 @@
     o0, a0, s0, b0, o1, a1, s1, b1,
     acts, acts_peer, w_cols, pre_act, grads, grads_peer, direct, grad_agg,
     c0, d0, e0, f0, c1, d1, e1, f1,
-    w_acc, wa_send, wa_recv, wb_send, wb_recv, wt_send,
+    w_acc, wa_send, wa_recv, wb_send, wb_recv,
     in_sem,
     sem_a0, sem_a1, sem_b0, sem_b1, sem_feat, sem_cols, sem_cols_core, sem_agg, sem_acts,
     sem_gather, sem_pass, sem_d0, sem_d1, sem_f0, sem_f1, sem_first, sem_second,
-    sem_third, sem_fourth, sem_swap,
+    sem_fourth, sem_swap,
 ):
     ny, nz, nx = dims
     ng = nz * CORES
@@ -97,8 +97,7 @@
     tile_count, tile_rows = tiles_in.shape[0], tiles_in.shape[1]
     dst_count = rows // tile_rows
     src_count = (rows + entries) // tile_rows
-    parts = nz // nx
-    band, piece = half // ny, width // parts
+    band = half // ny
 
     dom = lax.axis_index("dom")
     x = lax.axis_index("rep")
@@ -151,30 +150,9 @@
     greet(ng, g, at_g)
     greet(ny, y, at_y)
     greet(nx, x, at_x)
+    expected = (ng - 1) + (ny - 1) + (nx - 1)
 
     ways = (dict(n=ny, me=y, at=at_y), dict(n=nz, me=z, at=at_z))
-
-    def across(h, i, column):
-        return (ways[1 - h]["at"](i)[0], column)
-
-    def senders(h, step):
-        def one(k, carry):
-            i, column = x * parts + lax.div(k, nx), lax.rem(k, nx)
-
-            @pl.when(jnp.logical_or(i != ways[1 - h]["me"], column != x))
-            def _():
-                step(k, i, column)
-
-            return carry
-
-        lax.fori_loop(0, parts * nx, one, 0)
-
-    expected = (ng - 1) + (ny - 1) + (nx - 1)
-    for h in range(2):
-        senders(h, lambda k, i, column: greet_one(across(h, i, column)))
-        after = ways[1 - h]
-        mine = (lax.div(after["me"], parts) == x).astype(jnp.int32)
-        expected = expected + after["n"] - mine
 
     for f in fetches:
         f.start()
@@ -369,8 +347,10 @@
     def second(h):
         way = ways[1 - h]
         return Exchange(
-            way["n"], way["me"], way["at"], lambda p: wb_send.at[h, p],
-            lambda s, k: wb_recv.at[h, k - 1], *sem_pair(sem_second, h)
+            way["n"] * nx, way["me"] * nx + x,
+            lambda p: (way["at"](lax.div(p, nx))[0], lax.rem(p, nx)),
+            lambda p: wb_send.at[h, lax.rem(p, nx)], lambda s, k: wb_recv.at[h, s],
+            *sem_pair(sem_second, h)
         )
 
     seconds = [second(0), second(1)]
@@ -382,52 +362,9 @@
             total = w_acc[q, own_rows, :]
             for k in range(way["n"] - 1):
                 total = total + wa_recv[h, k, q].astype(F32)
-            for i in range(parts):
-                wb_send[h, q * parts + i] = total[:, i * piece : (i + 1) * piece]
+            wb_send[h, q] = total.astype(BF16)
         seconds[h].start()
-
-    scale = float(rows * nd) ** (-0.5)
-
-    def piece_at(h, i, column):
-        r = h * half + ways[h]["me"] * band
-        q = column * width + lax.rem(i, parts) * piece
-        return out_w.at[c, pl.ds(pl.multiple_of(r, band), band), pl.ds(pl.multiple_of(q, piece), piece)]
-
-    def third(h, k, dst, device, slot):
-        return pltpu.make_async_remote_copy(
-            src_ref=wt_send.at[h], dst_ref=dst, send_sem=sem_third.at[h, 0, k],
-            recv_sem=sem_third.at[h, 1, slot], device_id=device, device_id_type=MESH,
-        )
-
-    def thirds(h, step):
-        after = ways[1 - h]
-        me = after["me"]
-        slot = lax.rem(me, parts) * nx + x
-        target = lax.div(me, parts)
-
-        def one(k, carry):
-            copy = third(h, k, piece_at(h, me, x), across(h, lax.rem(me + k, after["n"]), target), slot)
-
-            @pl.when(jnp.logical_or(k != 0, target != x))
-            def _():
-                step(copy)
-
-            return carry
-
-        lax.fori_loop(0, after["n"], one, 0)
-
-    for h in range(2):
-        seconds[h].wait_recv()
-        after = ways[1 - h]
-        total = wb_send[h, after["me"]]
-        for k in range(after["n"] - 1):
-            total = total + wb_recv[h, k]
-        wt_send[h] = (total * scale).astype(BF16)
-        thirds(h, lambda copy: copy.start())
-
-        @pl.when(lax.div(after["me"], parts) == x)
-        def _():
-            piece_at(h, after["me"], x)[...] = wt_send[h]
+        wb_recv[h, after["me"] * nx + x] = wb_send[h, x]
 
     back_d0.wait_recv()
     e0[...] = dot(perm10[...], d0[...].reshape(entries, half)).astype(BF16).reshape(ng, per_g, half)
@@ -457,11 +394,15 @@
         )
 
     fourths = [fourth(0), fourth(1)]
+    scale = float(rows * nd) ** (-0.5)
     for h in range(2):
-        senders(
-            h,
-            lambda k, i, column: third(h, 0, piece_at(h, i, column), across(h, i, column), k).wait_recv(),
-        )
+        seconds[h].wait_recv()
+        mine = band_at(h, ways[h]["me"], c)
+        for q in range(nx):
+            total = wb_recv[h, q].astype(F32)
+            for i in range(1, ways[1 - h]["n"]):
+                total = total + wb_recv[h, i * nx + q].astype(F32)
+            mine[:, pl.ds(q * width, width)] = (total * scale).astype(BF16)
         fourths[h].start()
         swap(h, 0).start()
 
@@ -488,8 +429,6 @@
         return carry
 
     lax.fori_loop(0, ny, swapped, 0)
-    for h in range(2):
-        thirds(h, lambda copy: copy.wait_send())
     for done in (
         [out_a0, out_a1, out_b0, out_b1, feats, cols, cols_core, aggs, send_grads]
         + [gather, back_d0, back_d1, back_f0, back_f1] + send_acts + firsts + seconds + fourths
@@ -524,9 +463,8 @@
         entries = doms * slots
         tile_count, tile_rows = tiles.shape[0], tiles.shape[1]
         per_g, per_y = entries // ng, entries // ny
-        assert ny == nz and rows == width and nz % nx == 0
-        parts = nz // nx
-        band, piece = half // ny, width // parts
+        assert ny == nz and rows == width
+        band = half // ny
         vmem, stay = (pl.BlockSpec(memory_space=s) for s in (pltpu.VMEM, pl.ANY))
 
         def scratch(*shape, kind=BF16):
@@ -552,15 +490,14 @@
             by_y, by_y, by_g, by_g, by_g, by_g, by_y, by_y,
             scratch(nx, width, width, kind=F32),
             scratch(2, ny, nx, band, width), scratch(2, ny - 1, nx, band, width),
-            scratch(2, nz, band, piece, kind=F32), scratch(2, nz - 1, band, piece, kind=F32),
-            scratch(2, band, piece),
+            scratch(2, nx, band, width), scratch(2, nz * nx, band, width),
         ]
         semaphores = [
             pltpu.SemaphoreType.DMA((9,)),
             sems(ng - 1), sems(ny - 1), sems(ny - 1), sems(ng - 1),
             sems(nx - 1), sems(nx - 1), sems(1), sems(nx - 1), sems(nx),
             sems(nx - 1), sems(1), sems(ny - 1), sems(ng - 1), sems(ng - 1), sems(ny - 1),
-            sems(ny - 1, 2), sems(ny - 1, 2), sems(nz, 2), sems(ny - 1, 2), sems(ny, 2),
+            sems(ny - 1, 2), sems(nz * nx - 1, 2), sems(ny - 1, 2), sems(ny, 2),
         ]
         shapes = (
             jax.ShapeDtypeStruct((rows, width), BF16),

time: 74.2 us -> 74.9 us (level)
    pallas_call x1, Pallas kernels: 72.3 us -> 73.1 us  [local(): pl.pallas_call(functools.partial(kernel, (ny, nz, nx)), out_shape=tuple((...]
where the time goes in v5:
time: 74.9 us; the launch traced here: 74.8 us
  Pallas kernels  74.1 us (99%)
    pallas_call x1, Pallas kernels, local(): pl.pallas_call(functools.partial(kernel, (ny, nz, nx)), out_shape=tuple((...  73.1 us

profile of v5, /device:TPU:1, one launch (start us, length us, event | category | flops | bytes accessed | tf_op | source)
XLA Modules:
  0.0 74.8 jit_solution(11708627971070507510)
XLA Ops:
  0.6 73.1 %shard_map.120 = (bf16[256,256]{1,0:T(8,128)(2,1)S(1)}, bf16[256,256]{1,0:T(8,128)(2,1)S(1)}, bf16[2,256,1024]{2,1,0:T(8,128)(2,1)S(1)}) custom-call(bf16[256,256]{1,0:T(8,128)(2,1)} %feat_in.1, bf16[256,1024]{1,0:T(8,128)(2,1)} %w_self_in.1, bf16[256,1024]{1,0:T(8,128)(2,1)} %w_neigh_in.1, bf16[256,256]{1,0:T(8,128)(2,1)} %grad_out_in.1, s32[4,128]{1,0:T(4,128)} %bitcast.4, ...), custom_call_target="tpu_custom_call" | custom-call | tf_op jit(solution)/shard_map/pallas_call | solution.py:507
  73.7 1.1 %shard_map.121 = (bf16[256,256]{1,0:T(8,128)(2,1)}, bf16[256,256]{1,0:T(8,128)(2,1)}, bf16[256,1024]{1,0:T(8,128)(2,1)}, bf16[256,1024]{1,0:T(8,128)(2,1)}) custom-call(bf16[256,256]{1,0:T(8,128)(2,1)S(1)} %get-tuple-element.7.hidden, bf16[256,256]{1,0:T(8,128)(2,1)S(1)} %get-tuple-element.8.grad_feat, bf16[2,256,1024]{2,1,0:T(8,128)(2,1)S(1)} %get-tuple-element.9.both), custom_call_target="tpu_custom_call" | custom-call | tf_op jit(solution)/shard_map/pallas_call | solution.py:526

commit v6 on v4

--- a/solution.py
+++ b/solution.py
@@ -20,6 +20,10 @@
 
 def dot(a, b, dims=NN):
     return lax.dot_general(a, b, dims, preferred_element_type=F32)
+
+
+def far_first(n, j):
+    return n // 2 + lax.div(j + 1, 2) * (1 - 2 * lax.rem(j, 2))
 
 
 class Exchange:
@@ -54,8 +58,7 @@
             return
 
         def step(j, carry):
-            k = self.n // 2 + lax.div(j + 1, 2) * (1 - 2 * lax.rem(j, 2))
-            self.outgoing(k).start()
+            self.outgoing(far_first(self.n, j)).start()
             return carry
 
         lax.fori_loop(0, self.n - 1, step, 0)
@@ -77,7 +80,7 @@
     feat_in, w_self_in, w_neigh_in, grad_out_in, list_in, count_in, dst_in, src_in, tiles_in,
     hidden, grad_feat, out_w,
     weights, grad_out, list_t, count, tile_dst, tile_src, tiles,
-    perm01, perm10, hot0, hot1, edges, degree, table,
+    perm01, perm10, hot0, hot1, edges, edges_t, degree, own_sum,
     o0, a0, s0, b0, o1, a1, s1, b1,
     acts, acts_peer, w_cols, pre_act, grads, grads_peer, direct, grad_agg,
     c0, d0, e0, f0, c1, d1, e1, f1,
@@ -142,14 +145,14 @@
         pl.semaphore_signal(barrier, inc=1, device_id=device, device_id_type=MESH)
 
     def greet(n, me, device):
-        def step(k, carry):
-            greet_one(device(lax.rem(me + k, n)))
+        def step(j, carry):
+            greet_one(device(lax.rem(me + far_first(n, j), n)))
             return carry
 
-        lax.fori_loop(1, n, step, 0)
-
+        lax.fori_loop(0, n - 1, step, 0)
+
+    greet(ny, y, at_y)
     greet(ng, g, at_g)
-    greet(ny, y, at_y)
     greet(nx, x, at_x)
 
     ways = (dict(n=ny, me=y, at=at_y), dict(n=nz, me=z, at=at_z))
@@ -170,12 +173,6 @@
         lax.fori_loop(0, parts * nx, one, 0)
 
     expected = (ng - 1) + (ny - 1) + (nx - 1)
-    for h in range(2):
-        senders(h, lambda k, i, column: greet_one(across(h, i, column)))
-        after = ways[1 - h]
-        mine = (lax.div(after["me"], parts) == x).astype(jnp.int32)
-        expected = expected + after["n"] - mine
-
     for f in fetches:
         f.start()
 
@@ -240,7 +237,6 @@
     a0[g] = o0[g]
     a1[y] = o1[y]
     w_cols[c, x] = weights[c, :, columns(x)]
-    table[:rows, :] = feat
 
     y_out = lax.div(col, slots * ng)
     g_out = lax.rem(lax.div(col, slots), ng)
@@ -270,17 +266,21 @@
             edges[(1,) + at] = (total - top.astype(F32)).astype(BF16)
     ones = jnp.ones((rows + entries, tile_rows), BF16)
     degree[...] = jnp.maximum(dot(edges[0], ones) + dot(edges[1], ones), 1.0)
+    for i in range(2):
+        edges_t[i] = dot(edges[i, :, rows:], perm01[...]).astype(BF16)
+    own_sum[...] = dot(edges[0, :, :rows], feat) + dot(edges[1, :, :rows], feat)
     cols.wait_recv()
     cols_core.start()
 
+    safe = jnp.concatenate([degree[...]] * (width // tile_rows), axis=1)
     out_b0.wait_recv()
-    table[rows:, :half] = b0[...].reshape(entries, half)
+    mirrored = b0[...].reshape(entries, half)
+    left = dot(edges[0, :, rows:], mirrored) + dot(edges[1, :, rows:], mirrored)
+    acts[1, x, :, :half] = ((own_sum[:, :half] + left) / safe[:, :half]).astype(BF16)
     out_b1.wait_recv()
-    table[rows:, half:] = dot(perm01[...], b1[...].reshape(entries, half)).astype(BF16)
-
-    safe = jnp.concatenate([degree[...]] * (width // tile_rows), axis=1)
-    summed = dot(edges[0], table[...]) + dot(edges[1], table[...])
-    acts[1, x] = (summed / safe).astype(BF16)
+    mirrored = b1[...].reshape(entries, half)
+    right = dot(edges_t[0], mirrored) + dot(edges_t[1], mirrored)
+    acts[1, x, :, half:] = ((own_sum[:, half:] + right) / safe[:, half:]).astype(BF16)
     aggs = Exchange(
         nx, x, at_x, lambda p: acts.at[1, x], lambda s, k: acts.at[1, s], *sem_pair(sem_agg)
     )
@@ -326,9 +326,7 @@
         done.wait_recv()
     send_grads.wait_recv()
     for q in range(nx):
-        block = w_acc[q] + dot(acts_peer[q], grads_peer[...], TN)
-        w_acc[q] = block
-        block = block.astype(BF16)
+        block = (w_acc[q] + dot(acts_peer[q], grads_peer[...], TN)).astype(BF16)
         for h in range(2):
             wa_send[h, :, q] = block[h * half : (h + 1) * half, :].reshape(ny, band, width)
 
@@ -351,12 +349,11 @@
         direct[...] += dot(grads[q], weights[0, :, columns(q)], NT)
         grad_agg[...] += dot(grads[q], weights[1, :, columns(q)], NT)
     scaled = (grad_agg[...] / safe).astype(BF16)
-    table_grad = dot(edges[0], scaled, TN) + dot(edges[1], scaled, TN)
-    direct[...] += table_grad[:rows, :]
-    mirror = table_grad[rows:, :].astype(BF16)
-
-    c0[...] = mirror[:, :half].reshape(ny, per_y, half)
-    c1[...] = dot(perm10[...], mirror[:, half:]).astype(BF16).reshape(ng, per_g, half)
+    left, right = scaled[:, :half], scaled[:, half:]
+    left = dot(edges[0, :, rows:], left, TN) + dot(edges[1, :, rows:], left, TN)
+    right = dot(edges_t[0], right, TN) + dot(edges_t[1], right, TN)
+    c0[...] = left.astype(BF16).reshape(ny, per_y, half)
+    c1[...] = right.astype(BF16).reshape(ng, per_g, half)
     back_d0 = Exchange(ny, y, at_y, lambda p: c0.at[p], lambda s, k: d0.at[s], *sem_pair(sem_d0))
     back_d1 = Exchange(ng, g, at_g, lambda p: c1.at[p], lambda s, k: d1.at[s], *sem_pair(sem_d1))
     back_f0 = Exchange(ng, g, at_g, lambda p: e0.at[p], lambda s, k: f0.at[s], *sem_pair(sem_f0))
@@ -377,15 +374,16 @@
     for h in range(2):
         firsts[h].wait_recv()
         way, after = ways[h], ways[1 - h]
-        own_rows = pl.ds(pl.multiple_of(h * half + way["me"] * band, band), band)
         for q in range(nx):
-            total = w_acc[q, own_rows, :]
+            total = wa_send[h, way["me"], q].astype(F32)
             for k in range(way["n"] - 1):
                 total = total + wa_recv[h, k, q].astype(F32)
             for i in range(parts):
                 wb_send[h, q * parts + i] = total[:, i * piece : (i + 1) * piece]
         seconds[h].start()
 
+    direct[...] += dot(edges[0, :, :rows], scaled, TN) + dot(edges[1, :, :rows], scaled, TN)
+
     scale = float(rows * nd) ** (-0.5)
 
     def piece_at(h, i, column):
@@ -405,7 +403,8 @@
         slot = lax.rem(me, parts) * nx + x
         target = lax.div(me, parts)
 
-        def one(k, carry):
+        def one(j, carry):
+            k = far_first(after["n"], j)
             copy = third(h, k, piece_at(h, me, x), across(h, lax.rem(me + k, after["n"]), target), slot)
 
             @pl.when(jnp.logical_or(k != 0, target != x))
@@ -465,6 +464,13 @@
         fourths[h].start()
         swap(h, 0).start()
 
+    def pass_on(k):
+        for h in range(2):
+            fourths[h].wait_recv_one(k)
+            swap(h, k).start()
+
+    fourths[0].each(pass_on)
+
     back_f0.wait_recv()
     grad_feat[:, :half] = (
         direct[:, :half] + dot(hot0[...], f0[...].reshape(entries, half))
@@ -473,13 +479,6 @@
     grad_feat[:, half:] = (
         direct[:, half:] + dot(hot1[...], f1[...].reshape(entries, half))
     ).astype(BF16)
-
-    def pass_on(k):
-        for h in range(2):
-            fourths[h].wait_recv_one(k)
-            swap(h, k).start()
-
-    fourths[0].each(pass_on)
 
     def swapped(k, carry):
         for h in range(2):
@@ -543,8 +542,9 @@
             scratch(tile_count, tile_rows, tile_rows),
             scratch(entries, entries), scratch(entries, entries),
             scratch(rows, entries), scratch(rows, entries),
-            scratch(2, rows, rows + entries), scratch(rows, tile_rows, kind=F32),
-            scratch(rows + entries, width),
+            scratch(2, rows, rows + entries), scratch(2, rows, entries),
+            scratch(rows, tile_rows, kind=F32),
+            scratch(rows, width, kind=F32),
             by_g, by_g, by_y, by_y, by_y, by_y, by_g, by_g,
             scratch(2, nx, rows, width), scratch(nx, rows, width), scratch(2, nx, width, width),
             scratch(rows, width, kind=F32), scratch(nx, rows, width), scratch(rows, width),

time: 74.2 us -> 72.4 us (0.976)
  Pallas kernels: 73.4 us -> 71.6 us
    pallas_call x1, Pallas kernels: 72.3 us -> 70.5 us  [local(): pl.pallas_call(functools.partial(kernel, (ny, nz, nx)), out_shape=tuple((...]
where the time goes in v6:
time: 72.4 us; the launch traced here: 72.3 us
  Pallas kernels  71.6 us (99%)
    pallas_call x1, Pallas kernels, local(): pl.pallas_call(functools.partial(kernel, (ny, nz, nx)), out_shape=tuple((...  70.5 us

profile of v6, /device:TPU:1, one launch (start us, length us, event | category | flops | bytes accessed | tf_op | source)
XLA Modules:
  0.0 72.3 jit_solution(12706173985446772386)
XLA Ops:
  0.6 70.5 %shard_map.120 = (bf16[256,256]{1,0:T(8,128)(2,1)S(1)}, bf16[256,256]{1,0:T(8,128)(2,1)S(1)}, bf16[2,256,1024]{2,1,0:T(8,128)(2,1)S(1)}) custom-call(bf16[256,256]{1,0:T(8,128)(2,1)} %feat_in.1, bf16[256,1024]{1,0:T(8,128)(2,1)} %w_self_in.1, bf16[256,1024]{1,0:T(8,128)(2,1)} %w_neigh_in.1, bf16[256,256]{1,0:T(8,128)(2,1)} %grad_out_in.1, s32[4,128]{1,0:T(4,128)} %bitcast.4, ...), custom_call_target="tpu_custom_call" | custom-call | tf_op jit(solution)/shard_map/pallas_call | solution.py:570
  71.2 1.1 %shard_map.121 = (bf16[256,256]{1,0:T(8,128)(2,1)}, bf16[256,256]{1,0:T(8,128)(2,1)}, bf16[256,1024]{1,0:T(8,128)(2,1)}, bf16[256,1024]{1,0:T(8,128)(2,1)}) custom-call(bf16[256,256]{1,0:T(8,128)(2,1)S(1)} %get-tuple-element.7.hidden, bf16[256,256]{1,0:T(8,128)(2,1)S(1)} %get-tuple-element.8.grad_feat, bf16[2,256,1024]{2,1,0:T(8,128)(2,1)S(1)} %get-tuple-element.9.both), custom_call_target="tpu_custom_call" | custom-call | tf_op jit(solution)/shard_map/pallas_call | solution.py:589

commit v7 on v6

--- a/solution.py
+++ b/solution.py
@@ -22,8 +22,8 @@
     return lax.dot_general(a, b, dims, preferred_element_type=F32)
 
 
-def far_first(n, j):
-    return n // 2 + lax.div(j + 1, 2) * (1 - 2 * lax.rem(j, 2))
+def far_first(n):
+    return sorted(range(1, n), key=lambda k: -min(k, n - k))
 
 
 class Exchange:
@@ -43,25 +43,16 @@
         )
 
     def each(self, step):
-        if self.n == 2:
-            step(1)
-        else:
-            lax.fori_loop(1, self.n, lambda k, c: (step(k), c)[1], 0)
+        for k in reversed(far_first(self.n)):
+            step(k)
 
     def outgoing(self, k):
         peer = lax.rem(self.me + k, self.n)
         return self.copy(k, self.src(peer), self.dst(self.me, k), peer)
 
     def start(self):
-        if self.n == 2:
-            self.outgoing(1).start()
-            return
-
-        def step(j, carry):
-            self.outgoing(far_first(self.n, j)).start()
-            return carry
-
-        lax.fori_loop(0, self.n - 1, step, 0)
+        for k in far_first(self.n):
+            self.outgoing(k).start()
 
     def wait_send(self):
         self.each(lambda k: self.outgoing(k).wait_send())
@@ -145,11 +136,8 @@
         pl.semaphore_signal(barrier, inc=1, device_id=device, device_id_type=MESH)
 
     def greet(n, me, device):
-        def step(j, carry):
-            greet_one(device(lax.rem(me + far_first(n, j), n)))
-            return carry
-
-        lax.fori_loop(0, n - 1, step, 0)
+        for k in far_first(n):
+            greet_one(device(lax.rem(me + k, n)))
 
     greet(ny, y, at_y)
     greet(ng, g, at_g)
@@ -161,16 +149,15 @@
         return (ways[1 - h]["at"](i)[0], column)
 
     def senders(h, step):
-        def one(k, carry):
-            i, column = x * parts + lax.div(k, nx), lax.rem(k, nx)
+        def one(k):
+            i, column = x * parts + k // nx, k % nx
 
             @pl.when(jnp.logical_or(i != ways[1 - h]["me"], column != x))
             def _():
                 step(k, i, column)
 
-            return carry
-
-        lax.fori_loop(0, parts * nx, one, 0)
+        for k in range(parts * nx):
+            one(k)
 
     expected = (ng - 1) + (ny - 1) + (nx - 1)
     for f in fetches:
@@ -273,18 +260,24 @@
     cols_core.start()
 
     safe = jnp.concatenate([degree[...]] * (width // tile_rows), axis=1)
+    def gather_mean(h):
+        here = pl.ds(h * half, half)
+        return Exchange(
+            nx, x, at_x, lambda p: acts.at[1, x, :, here], lambda s, k: acts.at[1, s, :, here],
+            *sem_pair(sem_agg, h)
+        )
+
+    aggs = [gather_mean(0), gather_mean(1)]
     out_b0.wait_recv()
     mirrored = b0[...].reshape(entries, half)
     left = dot(edges[0, :, rows:], mirrored) + dot(edges[1, :, rows:], mirrored)
     acts[1, x, :, :half] = ((own_sum[:, :half] + left) / safe[:, :half]).astype(BF16)
+    aggs[0].start()
     out_b1.wait_recv()
     mirrored = b1[...].reshape(entries, half)
     right = dot(edges_t[0], mirrored) + dot(edges_t[1], mirrored)
     acts[1, x, :, half:] = ((own_sum[:, half:] + right) / safe[:, half:]).astype(BF16)
-    aggs = Exchange(
-        nx, x, at_x, lambda p: acts.at[1, x], lambda s, k: acts.at[1, s], *sem_pair(sem_agg)
-    )
-    aggs.start()
+    aggs[1].start()
 
     def pass_acts(k):
         q = lax.rem(x - k + nx, nx)
@@ -303,7 +296,8 @@
     pre_act[...] = total
     for k in range(1, nx):
         q = lax.rem(x - k + nx, nx)
-        aggs.wait_recv_one(k)
+        aggs[0].wait_recv_one(k)
+        aggs[1].wait_recv_one(k)
         send_acts[k].start()
         pre_act[...] += dot(acts[1, q], w_cols[1, q])
     value = pre_act[...]
@@ -403,17 +397,16 @@
         slot = lax.rem(me, parts) * nx + x
         target = lax.div(me, parts)
 
-        def one(j, carry):
-            k = far_first(after["n"], j)
+        def one(k):
             copy = third(h, k, piece_at(h, me, x), across(h, lax.rem(me + k, after["n"]), target), slot)
 
-            @pl.when(jnp.logical_or(k != 0, target != x))
-            def _():
+            if k != 0:
                 step(copy)
-
-            return carry
-
-        lax.fori_loop(0, after["n"], one, 0)
+            else:
+                pl.when(target != x)(lambda: step(copy))
+
+        for k in far_first(after["n"]) + [0]:
+            one(k)
 
     for h in range(2):
         seconds[h].wait_recv()
@@ -480,18 +473,15 @@
         direct[:, half:] + dot(hot1[...], f1[...].reshape(entries, half))
     ).astype(BF16)
 
-    def swapped(k, carry):
+    for k in range(ny):
         for h in range(2):
             swap(h, k).wait_recv()
             swap(h, k).wait_send()
-        return carry
-
-    lax.fori_loop(0, ny, swapped, 0)
     for h in range(2):
         thirds(h, lambda copy: copy.wait_send())
     for done in (
-        [out_a0, out_a1, out_b0, out_b1, feats, cols, cols_core, aggs, send_grads]
-        + [gather, back_d0, back_d1, back_f0, back_f1] + send_acts + firsts + seconds + fourths
+        [out_a0, out_a1, out_b0, out_b1, feats, cols, cols_core, send_grads]
+        + [gather, back_d0, back_d1, back_f0, back_f1] + aggs + send_acts + firsts + seconds + fourths
     ):
         done.wait_send()
 
@@ -558,7 +548,7 @@
         semaphores = [
             pltpu.SemaphoreType.DMA((9,)),
             sems(ng - 1), sems(ny - 1), sems(ny - 1), sems(ng - 1),
-            sems(nx - 1), sems(nx - 1), sems(1), sems(nx - 1), sems(nx),
+            sems(nx - 1), sems(nx - 1), sems(1), sems(nx - 1, 2), sems(nx),
             sems(nx - 1), sems(1), sems(ny - 1), sems(ng - 1), sems(ng - 1), sems(ny - 1),
             sems(ny - 1, 2), sems(ny - 1, 2), sems(nz, 2), sems(ny - 1, 2), sems(ny, 2),
         ]

time: 72.4 us -> 69.6 us (0.961)
  Pallas kernels: 71.6 us -> 68.8 us
    pallas_call x1, Pallas kernels: 70.5 us -> 67.7 us  [local(): pl.pallas_call(functools.partial(kernel, (ny, nz, nx)), out_shape=tuple((...]
where the time goes in v7:
time: 69.6 us; the launch traced here: 69.4 us
  Pallas kernels  68.8 us (99%)
    pallas_call x1, Pallas kernels, local(): pl.pallas_call(functools.partial(kernel, (ny, nz, nx)), out_shape=tuple((...  67.7 us

profile of v7, /device:TPU:1, one launch (start us, length us, event | category | flops | bytes accessed | tf_op | source)
XLA Modules:
  0.0 69.4 jit_solution(12603935508410004393)
XLA Ops:
  0.6 67.7 %shard_map.120 = (bf16[256,256]{1,0:T(8,128)(2,1)S(1)}, bf16[256,256]{1,0:T(8,128)(2,1)S(1)}, bf16[2,256,1024]{2,1,0:T(8,128)(2,1)S(1)}) custom-call(bf16[256,256]{1,0:T(8,128)(2,1)} %feat_in.1, bf16[256,1024]{1,0:T(8,128)(2,1)} %w_self_in.1, bf16[256,1024]{1,0:T(8,128)(2,1)} %w_neigh_in.1, bf16[256,256]{1,0:T(8,128)(2,1)} %grad_out_in.1, s32[4,128]{1,0:T(4,128)} %bitcast.4, ...), custom_call_target="tpu_custom_call" | custom-call | tf_op jit(solution)/shard_map/pallas_call | solution.py:560
  68.3 1.1 %shard_map.121 = (bf16[256,256]{1,0:T(8,128)(2,1)}, bf16[256,256]{1,0:T(8,128)(2,1)}, bf16[256,1024]{1,0:T(8,128)(2,1)}, bf16[256,1024]{1,0:T(8,128)(2,1)}) custom-call(bf16[256,256]{1,0:T(8,128)(2,1)S(1)} %get-tuple-element.7.hidden, bf16[256,256]{1,0:T(8,128)(2,1)S(1)} %get-tuple-element.8.grad_feat, bf16[2,256,1024]{2,1,0:T(8,128)(2,1)S(1)} %get-tuple-element.9.both), custom_call_target="tpu_custom_call" | custom-call | tf_op jit(solution)/shard_map/pallas_call | solution.py:579

commit v8 on v7

--- a/solution.py
+++ b/solution.py
@@ -231,12 +231,12 @@
     for f in fetches[5:]:
         f.wait()
 
+    out_a1.wait_recv()
+    s1[...] = dot(perm10[...], a1[...].reshape(entries, half)).astype(BF16).reshape(ng, per_g, half)
+    out_b1.start()
     out_a0.wait_recv()
     s0[...] = dot(perm01[...], a0[...].reshape(entries, half)).astype(BF16).reshape(ny, per_y, half)
     out_b0.start()
-    out_a1.wait_recv()
-    s1[...] = dot(perm10[...], a1[...].reshape(entries, half)).astype(BF16).reshape(ng, per_g, half)
-    out_b1.start()
     b0[y] = s0[y]
     b1[g] = s1[g]
 
@@ -457,13 +457,22 @@
         fourths[h].start()
         swap(h, 0).start()
 
+    for h in range(2):
+        thirds(h, lambda copy: copy.wait_send())
+    for done in (
+        [out_a0, out_a1, out_b0, out_b1, feats, cols, cols_core, send_grads, gather]
+        + [back_d0, back_d1] + aggs + send_acts + firsts + seconds
+    ):
+        done.wait_send()
+
     def pass_on(k):
         for h in range(2):
             fourths[h].wait_recv_one(k)
             swap(h, k).start()
 
-    fourths[0].each(pass_on)
-
+    near = far_first(ny)[::-1]
+    for k in near[: ny // 2]:
+        pass_on(k)
     back_f0.wait_recv()
     grad_feat[:, :half] = (
         direct[:, :half] + dot(hot0[...], f0[...].reshape(entries, half))
@@ -472,18 +481,16 @@
     grad_feat[:, half:] = (
         direct[:, half:] + dot(hot1[...], f1[...].reshape(entries, half))
     ).astype(BF16)
-
-    for k in range(ny):
+    back_f0.wait_send()
+    back_f1.wait_send()
+    for k in near[ny // 2 :]:
+        pass_on(k)
+    for done in fourths:
+        done.wait_send()
+    for k in [0] + near:
         for h in range(2):
+            swap(h, k).wait_send()
             swap(h, k).wait_recv()
-            swap(h, k).wait_send()
-    for h in range(2):
-        thirds(h, lambda copy: copy.wait_send())
-    for done in (
-        [out_a0, out_a1, out_b0, out_b1, feats, cols, cols_core, send_grads]
-        + [gather, back_d0, back_d1, back_f0, back_f1] + aggs + send_acts + firsts + seconds + fourths
-    ):
-        done.wait_send()
 
 
 def write_out(hidden, grad_feat, both, out0, out1, out2, out3, sem):

time: 69.6 us -> 69.5 us (level)
  no operation moved by 1% of the time
where the time goes in v8:
time: 69.5 us; the launch traced here: 69.3 us
  Pallas kernels  68.7 us (99%)
    pallas_call x1, Pallas kernels, local(): pl.pallas_call(functools.partial(kernel, (ny, nz, nx)), out_shape=tuple((...  67.6 us

profile of v8, /device:TPU:1, one launch (start us, length us, event | category | flops | bytes accessed | tf_op | source)
XLA Modules:
  0.0 69.3 jit_solution(6366846796589966760)
XLA Ops:
  0.6 67.6 %shard_map.120 = (bf16[256,256]{1,0:T(8,128)(2,1)S(1)}, bf16[256,256]{1,0:T(8,128)(2,1)S(1)}, bf16[2,256,1024]{2,1,0:T(8,128)(2,1)S(1)}) custom-call(bf16[256,256]{1,0:T(8,128)(2,1)} %feat_in.1, bf16[256,1024]{1,0:T(8,128)(2,1)} %w_self_in.1, bf16[256,1024]{1,0:T(8,128)(2,1)} %w_neigh_in.1, bf16[256,256]{1,0:T(8,128)(2,1)} %grad_out_in.1, s32[4,128]{1,0:T(4,128)} %bitcast.4, ...), custom_call_target="tpu_custom_call" | custom-call | tf_op jit(solution)/shard_map/pallas_call | solution.py:567
  68.2 1.1 %shard_map.121 = (bf16[256,256]{1,0:T(8,128)(2,1)}, bf16[256,256]{1,0:T(8,128)(2,1)}, bf16[256,1024]{1,0:T(8,128)(2,1)}, bf16[256,1024]{1,0:T(8,128)(2,1)}) custom-call(bf16[256,256]{1,0:T(8,128)(2,1)S(1)} %get-tuple-element.7.hidden, bf16[256,256]{1,0:T(8,128)(2,1)S(1)} %get-tuple-element.8.grad_feat, bf16[2,256,1024]{2,1,0:T(8,128)(2,1)S(1)} %get-tuple-element.9.both), custom_call_target="tpu_custom_call" | custom-call | tf_op jit(solution)/shard_map/pallas_call | solution.py:586
